TPU v7x, 32 devices: a whole 2x2x4 slice. The times are simulated.
32 devices in a mesh: shard: 4 (over z), ctx: 4 (over y, x), tp: 2 (over core).
Axes of the slice: x: 2, y: 2, z: 4, core: 2. Of those that a mesh axis runs over, the one named last changes fastest.
Arguments:
- tokens: bfloat16 [2, 4, 4096, 512], P(None, 'shard', 'ctx'), may hold values from -6 to 6
- cotangent: bfloat16 [2, 4, 4096, 512], P(None, 'shard', 'ctx'), may hold values from -6 to 6
- w_query: bfloat16 [512, 512], P('shard', 'tp'), may hold values from -0.25 to 0.25
- w_key: bfloat16 [512, 512], P('shard', 'tp'), may hold values from -0.25 to 0.25
- w_value: bfloat16 [512, 512], P('shard', 'tp'), may hold values from -0.25 to 0.25
- w_out: bfloat16 [512, 512], P('tp', 'shard'), may hold values from -6 to 6
- w_up: bfloat16 [512, 2048], P('shard', 'tp'), may hold values from -0.25 to 0.25
- w_down: bfloat16 [2048, 512], P('tp', 'shard'), may hold values from -0.125 to 0.125
- b_query: bfloat16 [8, 64], P('tp', 'shard'), may hold values from -3 to 3
- b_value: bfloat16 [8, 64], P('tp', 'shard'), may hold values from -3 to 3
- b_up: bfloat16 [8, 256], P('tp', 'shard'), may hold values from -3 to 3
- b_out: bfloat16 [512], P('shard'), may hold values from -3 to 3
- b_down: bfloat16 [512], P('shard'), may hold values from -3 to 3
- gain_attn: bfloat16 [512], P('shard'), may hold values from 0.099609375 to 1.8984375
- shift_attn: bfloat16 [512], P('shard'), may hold values from -3 to 3
- gain_ffn: bfloat16 [512], P('shard'), may hold values from 0.099609375 to 1.8984375
- shift_ffn: bfloat16 [512], P('shard'), may hold values from -3 to 3
Outputs:
- output: bfloat16 [2, 4, 4096, 512], P(None, 'shard', 'ctx')
- grad_tokens: bfloat16 [2, 4, 4096, 512], P(None, 'shard', 'ctx')
- grad_w_query: float32 [512, 512], P('shard', 'tp')
- grad_w_key: float32 [512, 512], P('shard', 'tp')
- grad_w_value: float32 [512, 512], P('shard', 'tp')
- grad_w_out: float32 [512, 512], P('tp', 'shard')
- grad_w_up: float32 [512, 2048], P('shard', 'tp')
- grad_w_down: float32 [2048, 512], P('tp', 'shard')
- grad_b_query: float32 [8, 64], P('tp', 'shard')
- grad_b_value: float32 [8, 64], P('tp', 'shard')
- grad_b_up: float32 [8, 256], P('tp', 'shard')
- grad_b_out: float32 [512], P('shard')
- grad_b_down: float32 [512], P('shard')
- grad_gain_attn: float32 [512], P('shard')
- grad_shift_attn: float32 [512], P('shard')
- grad_gain_ffn: float32 [512], P('shard')
- grad_shift_ffn: float32 [512], P('shard')
All inputs are finite; a program needn't handle non-finite values.
Results may differ from a plain program's by a relative error of at most 0.017.
Values may be sent and summed in bfloat16 or wider, within the bound.
A program may use at most 256 MiB of HBM per device.

v0:
```python
import math

import jax
import jax.numpy as jnp
from jax import lax
from jax.sharding import PartitionSpec as P

norm_eps = 1e-05


def product(left, right):
    return jnp.dot(left, right, preferred_element_type=jnp.float32)


def product_tn(left, right):
    return lax.dot_general(
        left, right, (((0,), (0,)), ((), ())), preferred_element_type=jnp.float32
    )


def product_nt(left, right):
    return lax.dot_general(
        left, right, (((1,), (1,)), ((), ())), preferred_element_type=jnp.float32
    )


def unit_norm(values):
    average = jnp.mean(values, axis=-1, keepdims=True)
    centred = values - average
    variance = jnp.mean(centred * centred, axis=-1, keepdims=True)
    inverse = lax.rsqrt(variance + norm_eps)
    return (centred * inverse, inverse)


def norm_back(grad_normed, unit_vals, inverse, gain):
    scaled = grad_normed * gain
    return inverse * (
        scaled
        - jnp.mean(scaled, axis=-1, keepdims=True)
        - unit_vals * jnp.mean(scaled * unit_vals, axis=-1, keepdims=True)
    )


def gelu_exact(values):
    return jax.nn.gelu(values, approximate=False)


def add_terms(left_terms, right_terms):
    return tuple(
        (first_term + second_term for first_term, second_term in zip(left_terms, right_terms))
    )


def gather_weights(shards):
    (
        w_query,
        w_key,
        w_value,
        w_out,
        w_up,
        w_down,
        b_query,
        b_value,
        b_up,
        b_out,
        b_down,
        gain_attn,
        shift_attn,
        gain_ffn,
        shift_ffn,
    ) = shards
    return (
        lax.all_gather(w_query, "shard", axis=0, tiled=True),
        lax.all_gather(w_key, "shard", axis=0, tiled=True),
        lax.all_gather(w_value, "shard", axis=0, tiled=True),
        lax.all_gather(w_out, "shard", axis=1, tiled=True),
        lax.all_gather(w_up, "shard", axis=0, tiled=True),
        lax.all_gather(w_down, "shard", axis=1, tiled=True),
        lax.all_gather(b_query, "shard", axis=1, tiled=True),
        lax.all_gather(b_value, "shard", axis=1, tiled=True),
        lax.all_gather(b_up, "shard", axis=1, tiled=True),
        lax.all_gather(b_out, "shard", axis=0, tiled=True),
        lax.all_gather(b_down, "shard", axis=0, tiled=True),
        lax.all_gather(gain_attn, "shard", axis=0, tiled=True),
        lax.all_gather(shift_attn, "shard", axis=0, tiled=True),
        lax.all_gather(gain_ffn, "shard", axis=0, tiled=True),
        lax.all_gather(shift_ffn, "shard", axis=0, tiled=True),
    )


def reduce_end(grads):
    (
        g_query,
        g_key,
        g_value,
        g_out,
        g_up,
        g_down,
        g_bquery,
        g_bvalue,
        g_bup,
        g_bout,
        g_bdown,
        g_gain_one,
        g_shift_one,
        g_gain_two,
        g_shift_two,
    ) = grads
    (
        p_query,
        p_key,
        p_value,
        p_out,
        p_up,
        p_down,
        p_bquery,
        p_bvalue,
        p_bup,
        p_bout,
        p_bdown,
        p_gain_one,
        p_shift_one,
        p_gain_two,
        p_shift_two,
    ) = (
        lax.psum_scatter(
            g_query.astype(jnp.bfloat16), "shard", scatter_dimension=0, tiled=True
        ).astype(jnp.float32),
        lax.psum_scatter(
            g_key.astype(jnp.bfloat16), "shard", scatter_dimension=0, tiled=True
        ).astype(jnp.float32),
        lax.psum_scatter(
            g_value.astype(jnp.bfloat16), "shard", scatter_dimension=0, tiled=True
        ).astype(jnp.float32),
        lax.psum_scatter(
            g_out.astype(jnp.bfloat16), "shard", scatter_dimension=1, tiled=True
        ).astype(jnp.float32),
        lax.psum_scatter(
            g_up.astype(jnp.bfloat16), "shard", scatter_dimension=0, tiled=True
        ).astype(jnp.float32),
        lax.psum_scatter(
            g_down.astype(jnp.bfloat16), "shard", scatter_dimension=1, tiled=True
        ).astype(jnp.float32),
        lax.psum_scatter(
            g_bquery.astype(jnp.bfloat16), "shard", scatter_dimension=1, tiled=True
        ).astype(jnp.float32),
        lax.psum_scatter(
            g_bvalue.astype(jnp.bfloat16), "shard", scatter_dimension=1, tiled=True
        ).astype(jnp.float32),
        lax.psum_scatter(
            g_bup.astype(jnp.bfloat16), "shard", scatter_dimension=1, tiled=True
        ).astype(jnp.float32),
        lax.psum_scatter(
            g_bout.astype(jnp.bfloat16), "shard", scatter_dimension=0, tiled=True
        ).astype(jnp.float32),
        lax.psum_scatter(
            g_bdown.astype(jnp.bfloat16), "shard", scatter_dimension=0, tiled=True
        ).astype(jnp.float32),
        lax.psum_scatter(
            g_gain_one.astype(jnp.bfloat16), "shard", scatter_dimension=0, tiled=True
        ).astype(jnp.float32),
        lax.psum_scatter(
            g_shift_one.astype(jnp.bfloat16), "shard", scatter_dimension=0, tiled=True
        ).astype(jnp.float32),
        lax.psum_scatter(
            g_gain_two.astype(jnp.bfloat16), "shard", scatter_dimension=0, tiled=True
        ).astype(jnp.float32),
        lax.psum_scatter(
            g_shift_two.astype(jnp.bfloat16), "shard", scatter_dimension=0, tiled=True
        ).astype(jnp.float32),
    )
    return (
        lax.psum(p_query.astype(jnp.bfloat16), "ctx").astype(jnp.float32),
        lax.psum(p_key.astype(jnp.bfloat16), "ctx").astype(jnp.float32),
        lax.psum(p_value.astype(jnp.bfloat16), "ctx").astype(jnp.float32),
        lax.psum(p_out.astype(jnp.bfloat16), "ctx").astype(jnp.float32),
        lax.psum(p_up.astype(jnp.bfloat16), "ctx").astype(jnp.float32),
        lax.psum(p_down.astype(jnp.bfloat16), "ctx").astype(jnp.float32),
        lax.psum(p_bquery.astype(jnp.bfloat16), "ctx").astype(jnp.float32),
        lax.psum(p_bvalue.astype(jnp.bfloat16), "ctx").astype(jnp.float32),
        lax.psum(p_bup.astype(jnp.bfloat16), "ctx").astype(jnp.float32),
        lax.psum(p_bout.astype(jnp.bfloat16), "ctx").astype(jnp.float32),
        lax.psum(p_bdown.astype(jnp.bfloat16), "ctx").astype(jnp.float32),
        lax.psum(p_gain_one.astype(jnp.bfloat16), "ctx").astype(jnp.float32),
        lax.psum(p_shift_one.astype(jnp.bfloat16), "ctx").astype(jnp.float32),
        lax.psum(p_gain_two.astype(jnp.bfloat16), "ctx").astype(jnp.float32),
        lax.psum(p_shift_two.astype(jnp.bfloat16), "ctx").astype(jnp.float32),
    )


def branch_total(part_sum):
    return lax.psum(part_sum, "tp")


def input_total(part_sum):
    return lax.psum(part_sum, "tp")


def attend_forward(query_rows, keys_all, values_all, head_count, score_scale):
    row_count = query_rows.shape[0]
    block_rows = min(512, row_count)
    query_blocks = query_rows.reshape(row_count // block_rows, block_rows, head_count, -1)
    key_heads = keys_all.reshape(keys_all.shape[0], head_count, -1)
    value_heads = values_all.reshape(values_all.shape[0], head_count, -1)

    def one_block(query_block):
        raw_scores = (
            jnp.einsum("qhd,khd->hqk", query_block, key_heads, preferred_element_type=jnp.float32)
            * score_scale
        )
        top_score = jnp.max(raw_scores, axis=-1, keepdims=True)
        exponent = jnp.exp(raw_scores - top_score)
        row_total = jnp.sum(exponent, axis=-1, keepdims=True)
        attn_weights = (exponent / row_total).astype(jnp.bfloat16)
        mixed_block = jnp.einsum(
            "hqk,khd->qhd", attn_weights, value_heads, preferred_element_type=jnp.float32
        )
        return (mixed_block.astype(jnp.bfloat16), (top_score + jnp.log(row_total))[:, :, 0])

    mixed_rows, log_total = lax.map(one_block, query_blocks)
    return (mixed_rows.reshape(row_count, -1), log_total)


def attend_back(query_rows, keys_all, values_all, grad_mixed, log_total, head_count, score_scale):
    row_count = query_rows.shape[0]
    block_rows = min(512, row_count)
    block_count = row_count // block_rows
    query_blocks = query_rows.reshape(block_count, block_rows, head_count, -1)
    grad_blocks = grad_mixed.reshape(block_count, block_rows, head_count, -1)
    key_heads = keys_all.reshape(keys_all.shape[0], head_count, -1)
    value_heads = values_all.reshape(values_all.shape[0], head_count, -1)

    def one_block(carried, inputs):
        grad_keys, grad_values = carried
        query_block, grad_block, log_block = inputs
        raw_scores = (
            jnp.einsum("qhd,khd->hqk", query_block, key_heads, preferred_element_type=jnp.float32)
            * score_scale
        )
        prob_rows = jnp.exp(raw_scores - log_block[:, :, None])
        grad_probs = jnp.einsum(
            "qhd,khd->hqk", grad_block, value_heads, preferred_element_type=jnp.float32
        )
        grad_values = grad_values + jnp.einsum(
            "hqk,qhd->khd",
            prob_rows.astype(jnp.bfloat16),
            grad_block,
            preferred_element_type=jnp.float32,
        )
        row_delta = jnp.sum(grad_probs * prob_rows, axis=-1, keepdims=True)
        grad_scores = (prob_rows * (grad_probs - row_delta)).astype(jnp.bfloat16)
        grad_query = (
            jnp.einsum("hqk,khd->qhd", grad_scores, key_heads, preferred_element_type=jnp.float32)
            * score_scale
        )
        grad_keys = (
            grad_keys
            + jnp.einsum(
                "hqk,qhd->khd", grad_scores, query_block, preferred_element_type=jnp.float32
            )
            * score_scale
        )
        return ((grad_keys, grad_values), grad_query)

    empty = jnp.zeros(key_heads.shape, jnp.float32)
    (grad_keys, grad_values), grad_query = lax.scan(
        one_block, (empty, empty), (query_blocks, grad_blocks, log_total)
    )
    return (
        grad_query.reshape(row_count, -1),
        grad_keys.reshape(grad_keys.shape[0], -1),
        grad_values.reshape(grad_values.shape[0], -1),
    )


def body(
    tokens,
    cotangent,
    w_query,
    w_key,
    w_value,
    w_out,
    w_up,
    w_down,
    b_query,
    b_value,
    b_up,
    b_out,
    b_down,
    gain_attn,
    shift_attn,
    gain_ffn,
    shift_ffn,
):
    shards = (
        w_query,
        w_key,
        w_value,
        w_out,
        w_up,
        w_down,
        b_query,
        b_value,
        b_up,
        b_out,
        b_down,
        gain_attn,
        shift_attn,
        gain_ffn,
        shift_ffn,
    )
    head_count = b_query.shape[0]
    head_width = b_query.shape[1] * lax.axis_size("shard")
    score_scale = 1.0 / math.sqrt(head_width)
    results = []
    input_grads = []
    local_sums = None
    for micro in range(tokens.shape[0]):
        front = gather_weights(shards)
        (
            mat_query,
            mat_key,
            mat_value,
            mat_out,
            mat_up,
            mat_down,
            vec_query,
            vec_value,
            vec_up,
            vec_out,
            vec_down,
            gain_one,
            shift_one,
            gain_two,
            shift_two,
        ) = front
        gain_one_f = gain_one.astype(jnp.float32)
        gain_two_f = gain_two.astype(jnp.float32)
        x_input = tokens[micro, 0].astype(jnp.float32)
        unit_one, inverse_one = unit_norm(x_input)
        normed_one = (unit_one * gain_one_f + shift_one.astype(jnp.float32)).astype(jnp.bfloat16)
        query_rows = (
            product(normed_one, mat_query) + vec_query.astype(jnp.float32).reshape(-1)
        ).astype(jnp.bfloat16)
        key_local = product(normed_one, mat_key).astype(jnp.bfloat16)
        value_local = (
            product(normed_one, mat_value) + vec_value.astype(jnp.float32).reshape(-1)
        ).astype(jnp.bfloat16)
        keys_all, values_all = (
            lax.all_gather(key_local, "ctx", axis=0, tiled=True),
            lax.all_gather(value_local, "ctx", axis=0, tiled=True),
        )
        mixed_rows, log_total = attend_forward(
            query_rows, keys_all, values_all, head_count, score_scale
        )
        attended = branch_total(product(mixed_rows, mat_out)) + vec_out.astype(jnp.float32)
        middle = x_input + attended
        unit_two, inverse_two = unit_norm(middle)
        normed_two = (unit_two * gain_two_f + shift_two.astype(jnp.float32)).astype(jnp.bfloat16)
        pre_active = product(normed_two, mat_up) + vec_up.astype(jnp.float32).reshape(-1)
        active_f, gelu_pull = jax.vjp(gelu_exact, pre_active)
        active = active_f.astype(jnp.bfloat16)
        ffn_out = branch_total(product(active, mat_down)) + vec_down.astype(jnp.float32)
        results.append((middle + ffn_out).astype(jnp.bfloat16))
        back = gather_weights(shards)
        upstream_b = cotangent[micro, 0]
        upstream = upstream_b.astype(jnp.float32)
        grad_w_down = product_tn(active, upstream_b)
        grad_b_down = jnp.sum(upstream, axis=0)
        grad_active = product_nt(upstream_b, back[5])
        grad_pre = gelu_pull(grad_active)[0].astype(jnp.bfloat16)
        grad_w_up = product_tn(normed_two, grad_pre)
        grad_b_up = jnp.sum(grad_pre.astype(jnp.float32), axis=0).reshape(head_count, -1)
        grad_normed_two = input_total(product_nt(grad_pre, back[4]))
        grad_gain_two = jnp.sum(grad_normed_two * unit_two, axis=0)
        grad_shift_two = jnp.sum(grad_normed_two, axis=0)
        grad_middle = upstream + norm_back(
            grad_normed_two, unit_two, inverse_two, back[13].astype(jnp.float32)
        )
        grad_att = grad_middle.astype(jnp.bfloat16)
        grad_b_out = jnp.sum(grad_att.astype(jnp.float32), axis=0)
        grad_w_out = product_tn(mixed_rows, grad_att)
        grad_mixed = product_nt(grad_att, back[3]).astype(jnp.bfloat16)
        grad_query, grad_keys_all, grad_values_all = attend_back(
            query_rows, keys_all, values_all, grad_mixed, log_total, head_count, score_scale
        )
        grad_keys_mine, grad_values_mine = (
            lax.psum_scatter(
                grad_keys_all.astype(jnp.bfloat16), "ctx", scatter_dimension=0, tiled=True
            ).astype(jnp.float32),
            lax.psum_scatter(
                grad_values_all.astype(jnp.bfloat16), "ctx", scatter_dimension=0, tiled=True
            ).astype(jnp.float32),
        )
        grad_query_b = grad_query.astype(jnp.bfloat16)
        grad_key_b = grad_keys_mine.astype(jnp.bfloat16)
        grad_value_b = grad_values_mine.astype(jnp.bfloat16)
        grad_w_query = product_tn(normed_one, grad_query_b)
        grad_w_key = product_tn(normed_one, grad_key_b)
        grad_w_value = product_tn(normed_one, grad_value_b)
        grad_b_query = jnp.sum(grad_query_b.astype(jnp.float32), axis=0).reshape(head_count, -1)
        grad_b_value = jnp.sum(grad_value_b.astype(jnp.float32), axis=0).reshape(head_count, -1)
        grad_normed_one = input_total(
            product_nt(grad_query_b, back[0])
            + product_nt(grad_key_b, back[1])
            + product_nt(grad_value_b, back[2])
        )
        grad_gain_one = jnp.sum(grad_normed_one * unit_one, axis=0)
        grad_shift_one = jnp.sum(grad_normed_one, axis=0)
        grad_input = grad_middle + norm_back(
            grad_normed_one, unit_one, inverse_one, back[11].astype(jnp.float32)
        )
        input_grads.append(grad_input.astype(jnp.bfloat16))
        micro_grads = (
            grad_w_query,
            grad_w_key,
            grad_w_value,
            grad_w_out,
            grad_w_up,
            grad_w_down,
            grad_b_query,
            grad_b_value,
            grad_b_up,
            grad_b_out,
            grad_b_down,
            grad_gain_one,
            grad_shift_one,
            grad_gain_two,
            grad_shift_two,
        )
        local_sums = micro_grads if local_sums is None else add_terms(local_sums, micro_grads)
    final_grads = reduce_end(local_sums)
    output = jnp.stack(results)[:, None]
    grad_tokens = jnp.stack(input_grads)[:, None]
    return (
        output,
        grad_tokens,
        final_grads[0],
        final_grads[1],
        final_grads[2],
        final_grads[3],
        final_grads[4],
        final_grads[5],
        final_grads[6],
        final_grads[7],
        final_grads[8],
        final_grads[9],
        final_grads[10],
        final_grads[11],
        final_grads[12],
        final_grads[13],
        final_grads[14],
    )


def solution(mesh):
    return jax.shard_map(
        body,
        mesh=mesh,
        in_specs=(
            P(None, "shard", "ctx", None),
            P(None, "shard", "ctx", None),
            P("shard", "tp"),
            P("shard", "tp"),
            P("shard", "tp"),
            P("tp", "shard"),
            P("shard", "tp"),
            P("tp", "shard"),
            P("tp", "shard"),
            P("tp", "shard"),
            P("tp", "shard"),
            P("shard"),
            P("shard"),
            P("shard"),
            P("shard"),
            P("shard"),
            P("shard"),
        ),
        out_specs=(
            P(None, "shard", "ctx", None),
            P(None, "shard", "ctx", None),
            P("shard", "tp"),
            P("shard", "tp"),
            P("shard", "tp"),
            P("tp", "shard"),
            P("shard", "tp"),
            P("tp", "shard"),
            P("tp", "shard"),
            P("tp", "shard"),
            P("tp", "shard"),
            P("shard"),
            P("shard"),
            P("shard"),
            P("shard"),
            P("shard"),
            P("shard"),
        ),
        check_vma=False,
    )
```

profile of v0, /device:TPU:0, one launch (start us, length us, event | category | flops | bytes accessed | tf_op | source)
XLA Modules:
  0.0 1317.2 jit_solution(13096622181151597219)
XLA Ops:
  133.0 84.9 %while.54 = (s32[]{:T(128)}, bf16[2,512,4,64]{1,3,2,0:T(8,128)(2,1)S(1)}, f32[2,4,512]{2,1,0:T(4,128)S(1)}, bf16[2,512,4,64]{1,3,2,0:T(8,128)(2,1)S(1)}, bf16[40...) while((s32[]{:T(128)}, bf16[2,512,4,64]{1,3,2,0:T(8,128)(2,1)S(1)}, ...), condition=%wide.region_5.6_spmd, body=%wide.region_2.5_spmd.sunk | while | flops 2223110144 | bytes 105447504 | solution.py:220
  160.9 14.8 %fusion.305 = bf16[2,512,4,64]{1,3,2,0:T(8,128)(2,1)S(1)} fusion(bf16[2,512,4,64]{1,3,2,0:T(8,128)(2,1)S(1)} %get-tuple-element.781, s32[]{:T(128)} %get-tuple-element.780, bf16[4096,4,64]{0,2,1:T(8,128)(2,1)} %get-tuple-element.792, f32[4,512,4096]{2,1,0:T(8,128)} %get-tuple-element.720, f32[4,512]{1,0:T(4,128)S(1)} %fusion.304, ...), kind=kOutput, calls=%fused_computation.7.clone.1 | convolution fusion | flops 1107427328 | bytes 35930116 | tf_op jit(solution)/shard_map/while/body/eval_jaxpr/hqk,khd->qhd/dot_general | solution.py:215
  203.2 14.8 %fusion.305 = bf16[2,512,4,64]{1,3,2,0:T(8,128)(2,1)S(1)} fusion(bf16[2,512,4,64]{1,3,2,0:T(8,128)(2,1)S(1)} %get-tuple-element.781, s32[]{:T(128)} %get-tuple-element.780, bf16[4096,4,64]{0,2,1:T(8,128)(2,1)} %get-tuple-element.792, f32[4,512,4096]{2,1,0:T(8,128)} %get-tuple-element.720, f32[4,512]{1,0:T(4,128)S(1)} %fusion.304, ...), kind=kOutput, calls=%fused_computation.7.clone.1 | convolution fusion | flops 1107427328 | bytes 35930116 | tf_op jit(solution)/shard_map/while/body/eval_jaxpr/hqk,khd->qhd/dot_general | solution.py:215
  226.8 84.4 %while.55 = (s32[]{:T(128)}, bf16[2,512,4,64]{1,3,2,0:T(8,128)(2,1)S(1)}, f32[2,4,512]{2,1,0:T(4,128)S(1)}, bf16[2,512,4,64]{1,3,2,0:T(8,128)(2,1)S(1)}, bf16[40...) while((s32[]{:T(128)}, bf16[2,512,4,64]{1,3,2,0:T(8,128)(2,1)S(1)}, ...), condition=%wide.region_15.16_spmd, body=%wide.region_12.15_spmd.sunk | while | flops 2223110144 | bytes 105447504 | solution.py:220
  296.4 14.8 %fusion.309 = bf16[2,512,4,64]{1,3,2,0:T(8,128)(2,1)S(1)} fusion(bf16[2,512,4,64]{1,3,2,0:T(8,128)(2,1)S(1)} %get-tuple-element.760, s32[]{:T(128)} %get-tuple-element.759, bf16[4096,4,64]{0,2,1:T(8,128)(2,1)} %get-tuple-element.771, f32[4,512,4096]{2,1,0:T(8,128)} %get-tuple-element.728, f32[4,512]{1,0:T(4,128)S(1)} %fusion.308, ...), kind=kOutput, calls=%fused_computation.21.clone.1 | convolution fusion | flops 1107427328 | bytes 35930116 | tf_op jit(solution)/shard_map/while/body/eval_jaxpr/hqk,khd->qhd/dot_general | solution.py:215
  364.7 21.7 %multiply_convert_fusion.3 = (bf16[1024,1024]{1,0:T(8,128)(2,1)}, f32[1024,1024]{1,0:T(8,128)}, bf16[1024,1024]{1,0:T(8,128)(2,1)}, f32[1024,1024]{1,0:T(8,128)}, f32[1024,1024]{1,0:T(8,128)}) fusion(f32[1024]{0:T(1024)S(1)} %bitcast.466, f32[1024,1024]{1,0:T(8,128)S(1)} %fusion.177, bf16[512,1024]{1,0:T(8,128)(2,1)S(1)} %copy-done.115, ...), kind=kOutput, calls=%fused_computation.111 | convolution fusion | flops 1214775296 | bytes 24133632 | tf_op jit(solution)/shard_map/dot_general | solution.py:12
  405.8 27.1 %all-reduce.19.cloned.1.call-done = (f32[1024,512]{1,0:T(8,128)}, f32[1024,512]{1,0:T(8,128)}) async-done(((f32[1024,512]{1,0:T(8,128)}, f32[1024,512]{1,0:T(8,128)}), (f32[1024,512]{1,0:T(8,128)}, f32[1024,512]{1,0:T(8,128)})) %all-reduce.19.cloned.1.call-update) | async-done | bytes 4194320 | tf_op jit(solution)/shard_map/psum | solution.py:196
  448.5 197.6 %while.56 = (s32[]{:T(128)}, f32[4096,4,64]{0,2,1:T(8,128)}, f32[4096,4,64]{0,2,1:T(8,128)}, bf16[2,512,4,64]{1,3,2,0:T(8,128)(2,1)}, bf16[2,512,4,64]{1,3,2,0:T...) while((s32[]{:T(128)}, f32[4096,4,64]{0,2,1:T(8,128)}, ...), condition=%wide.region_25.26_spmd.clone, body=%wide.region_23.25_spmd.clone.sunk | while | flops 5474744320 | bytes 351856320 | solution.py:266
  462.1 22.9 %multiply_reduce_fusion.20 = (f32[4,512]{1,0:T(4,128)S(1)}, f32[4,512,4096]{2,1,0:T(8,128)}) fusion(f32[4,512,4096]{2,1,0:T(8,128)} %fusion.319, f32[4,512]{1,0:T(4,128)S(1)} %dynamic-slice_bitcast_fusion.4, bf16[4096,4,64]{0,2,1:T(8,128)(2,1)S(1)} %copy-done.7, bf16[2,512,4,64]{1,3,2,0:T(8,128)(2,1)} %get-tuple-element.856, s32[]{:T(128)} %get-tuple-element.838), kind=kOutput, calls=%fused_computation.29.clone.1 | convolution fusion | flops 1107294208 | bytes 69485056 | tf_op jit(solution)/shard_map/while/body/eval_jaxpr/qhd,khd->hqk/dot_general | solution.py:241
  485.0 27.5 %multiply_convert_fusion.6 = bf16[4,512,4096]{2,1,0:T(8,128)(2,1)} fusion(f32[4,512,4096]{2,1,0:T(8,128)} %get-tuple-element.739, f32[4,512,4096]{2,1,0:T(8,128)} %fusion.319, f32[4,512]{1,0:T(4,128)S(1)} %get-tuple-element.740, f32[4,512]{1,0:T(4,128)S(1)} %dynamic-slice_bitcast_fusion.4), kind=kLoop, calls=%fused_computation.28.clone.1 | loop fusion | flops 41943040 | bytes 83902464 | tf_op jit(solution)/shard_map/while/body/eval_jaxpr/convert_element_type | solution.py:251
  530.4 15.9 %fusion.321 = f32[4096,4,64]{0,2,1:T(8,128)} fusion(f32[4,512,4096]{2,1,0:T(8,128)} %fusion.319, f32[4,512]{1,0:T(4,128)S(1)} %dynamic-slice_bitcast_fusion.4, f32[4096,4,64]{0,2,1:T(8,128)} %get-tuple-element.840, pred[]{:T(512)S(6)} %compare.6, bf16[2,512,4,64]{1,3,2,0:T(8,128)(2,1)} %get-tuple-element.856, s32[]{:T(128)} %get-tuple-element.838), kind=kOutput, calls=%fused_computation.39.clone.1 | convolution fusion | flops 1101004800 | bytes 42213888 | tf_op jit(solution)/shard_map/while/body/eval_jaxpr/hqk,qhd->khd/dot_general | solution.py:244
  559.5 22.9 %multiply_reduce_fusion.20 = (f32[4,512]{1,0:T(4,128)S(1)}, f32[4,512,4096]{2,1,0:T(8,128)}) fusion(f32[4,512,4096]{2,1,0:T(8,128)} %fusion.319, f32[4,512]{1,0:T(4,128)S(1)} %dynamic-slice_bitcast_fusion.4, bf16[4096,4,64]{0,2,1:T(8,128)(2,1)S(1)} %copy-done.7, bf16[2,512,4,64]{1,3,2,0:T(8,128)(2,1)} %get-tuple-element.856, s32[]{:T(128)} %get-tuple-element.838), kind=kOutput, calls=%fused_computation.29.clone.1 | convolution fusion | flops 1107294208 | bytes 69485056 | tf_op jit(solution)/shard_map/while/body/eval_jaxpr/qhd,khd->hqk/dot_general | solution.py:241
  582.4 27.5 %multiply_convert_fusion.6 = bf16[4,512,4096]{2,1,0:T(8,128)(2,1)} fusion(f32[4,512,4096]{2,1,0:T(8,128)} %get-tuple-element.739, f32[4,512,4096]{2,1,0:T(8,128)} %fusion.319, f32[4,512]{1,0:T(4,128)S(1)} %get-tuple-element.740, f32[4,512]{1,0:T(4,128)S(1)} %dynamic-slice_bitcast_fusion.4), kind=kLoop, calls=%fused_computation.28.clone.1 | loop fusion | flops 41943040 | bytes 83902464 | tf_op jit(solution)/shard_map/while/body/eval_jaxpr/convert_element_type | solution.py:251
  629.0 17.1 %fusion.321 = f32[4096,4,64]{0,2,1:T(8,128)} fusion(f32[4,512,4096]{2,1,0:T(8,128)} %fusion.319, f32[4,512]{1,0:T(4,128)S(1)} %dynamic-slice_bitcast_fusion.4, f32[4096,4,64]{0,2,1:T(8,128)} %get-tuple-element.840, pred[]{:T(512)S(6)} %compare.6, bf16[2,512,4,64]{1,3,2,0:T(8,128)(2,1)} %get-tuple-element.856, s32[]{:T(128)} %get-tuple-element.838), kind=kOutput, calls=%fused_computation.39.clone.1 | convolution fusion | flops 1101004800 | bytes 42213888 | tf_op jit(solution)/shard_map/while/body/eval_jaxpr/hqk,qhd->khd/dot_general | solution.py:244
  658.9 198.2 %while.57 = (s32[]{:T(128)}, f32[4096,4,64]{0,2,1:T(8,128)}, f32[4096,4,64]{0,2,1:T(8,128)}, bf16[2,512,4,64]{1,3,2,0:T(8,128)(2,1)}, bf16[2,512,4,64]{1,3,2,0:T...) while((s32[]{:T(128)}, f32[4096,4,64]{0,2,1:T(8,128)}, ...), condition=%wide.region_36.37_spmd.clone, body=%wide.region_34.36_spmd.clone.sunk | while | flops 5474744320 | bytes 351856320 | solution.py:266
  672.9 23.1 %multiply_reduce_fusion.21 = (f32[4,512]{1,0:T(4,128)S(1)}, f32[4,512,4096]{2,1,0:T(8,128)}) fusion(f32[4,512,4096]{2,1,0:T(8,128)} %fusion.332, f32[4,512]{1,0:T(4,128)S(1)} %dynamic-slice_bitcast_fusion.5, bf16[4096,4,64]{0,2,1:T(8,128)(2,1)S(1)} %copy-done.6, bf16[2,512,4,64]{1,3,2,0:T(8,128)(2,1)} %get-tuple-element.823, s32[]{:T(128)} %get-tuple-element.805), kind=kOutput, calls=%fused_computation.60.clone.1 | convolution fusion | flops 1107294208 | bytes 69485056 | tf_op jit(solution)/shard_map/while/body/eval_jaxpr/qhd,khd->hqk/dot_general | solution.py:241
  695.9 27.5 %multiply_convert_fusion.7 = bf16[4,512,4096]{2,1,0:T(8,128)(2,1)} fusion(f32[4,512,4096]{2,1,0:T(8,128)} %get-tuple-element.750, f32[4,512,4096]{2,1,0:T(8,128)} %fusion.332, f32[4,512]{1,0:T(4,128)S(1)} %get-tuple-element.751, f32[4,512]{1,0:T(4,128)S(1)} %dynamic-slice_bitcast_fusion.5), kind=kLoop, calls=%fused_computation.59.clone.1 | loop fusion | flops 41943040 | bytes 83902464 | tf_op jit(solution)/shard_map/while/body/eval_jaxpr/convert_element_type | solution.py:251
  741.3 15.9 %fusion.334 = f32[4096,4,64]{0,2,1:T(8,128)} fusion(f32[4,512,4096]{2,1,0:T(8,128)} %fusion.332, f32[4,512]{1,0:T(4,128)S(1)} %dynamic-slice_bitcast_fusion.5, f32[4096,4,64]{0,2,1:T(8,128)} %get-tuple-element.807, pred[]{:T(512)S(6)} %compare.7, bf16[2,512,4,64]{1,3,2,0:T(8,128)(2,1)} %get-tuple-element.823, s32[]{:T(128)} %get-tuple-element.805), kind=kOutput, calls=%fused_computation.70.clone.1 | convolution fusion | flops 1101004800 | bytes 42213888 | tf_op jit(solution)/shard_map/while/body/eval_jaxpr/hqk,qhd->khd/dot_general | solution.py:244
  770.3 22.9 %multiply_reduce_fusion.21 = (f32[4,512]{1,0:T(4,128)S(1)}, f32[4,512,4096]{2,1,0:T(8,128)}) fusion(f32[4,512,4096]{2,1,0:T(8,128)} %fusion.332, f32[4,512]{1,0:T(4,128)S(1)} %dynamic-slice_bitcast_fusion.5, bf16[4096,4,64]{0,2,1:T(8,128)(2,1)S(1)} %copy-done.6, bf16[2,512,4,64]{1,3,2,0:T(8,128)(2,1)} %get-tuple-element.823, s32[]{:T(128)} %get-tuple-element.805), kind=kOutput, calls=%fused_computation.60.clone.1 | convolution fusion | flops 1107294208 | bytes 69485056 | tf_op jit(solution)/shard_map/while/body/eval_jaxpr/qhd,khd->hqk/dot_general | solution.py:241
  793.3 27.5 %multiply_convert_fusion.7 = bf16[4,512,4096]{2,1,0:T(8,128)(2,1)} fusion(f32[4,512,4096]{2,1,0:T(8,128)} %get-tuple-element.750, f32[4,512,4096]{2,1,0:T(8,128)} %fusion.332, f32[4,512]{1,0:T(4,128)S(1)} %get-tuple-element.751, f32[4,512]{1,0:T(4,128)S(1)} %dynamic-slice_bitcast_fusion.5), kind=kLoop, calls=%fused_computation.59.clone.1 | loop fusion | flops 41943040 | bytes 83902464 | tf_op jit(solution)/shard_map/while/body/eval_jaxpr/convert_element_type | solution.py:251
  839.8 17.1 %fusion.334 = f32[4096,4,64]{0,2,1:T(8,128)} fusion(f32[4,512,4096]{2,1,0:T(8,128)} %fusion.332, f32[4,512]{1,0:T(4,128)S(1)} %dynamic-slice_bitcast_fusion.5, f32[4096,4,64]{0,2,1:T(8,128)} %get-tuple-element.807, pred[]{:T(512)S(6)} %compare.7, bf16[2,512,4,64]{1,3,2,0:T(8,128)(2,1)} %get-tuple-element.823, s32[]{:T(128)} %get-tuple-element.805), kind=kOutput, calls=%fused_computation.70.clone.1 | convolution fusion | flops 1101004800 | bytes 42213888 | tf_op jit(solution)/shard_map/while/body/eval_jaxpr/hqk,qhd->khd/dot_general | solution.py:244
  899.8 35.7 %reduce-scatter.24.cloned.1.call-done = bf16[1024,256]{0,1:T(8,128)(2,1)} async-done(((bf16[4096,256]{0,1:T(8,128)(2,1)}), bf16[1024,256]{0,1:T(8,128)(2,1)}) %reduce-scatter.24.cloned.1.call-update) | async-done | bytes 524304 | tf_op jit(solution)/shard_map/reduce_scatter | solution.py:388
  938.2 35.9 %reduce-scatter.28.cloned.1.call-done = bf16[1024,256]{0,1:T(8,128)(2,1)} async-done(((bf16[4096,256]{0,1:T(8,128)(2,1)}), bf16[1024,256]{0,1:T(8,128)(2,1)}) %reduce-scatter.28.cloned.1.call-update) | async-done | bytes 524304 | tf_op jit(solution)/shard_map/reduce_scatter | solution.py:388
  984.9 18.8 %reduce-scatter.42.cloned.1.call-done = bf16[128,1024]{1,0:T(8,128)(2,1)} async-done(((bf16[512,1024]{1,0:T(8,128)(2,1)}), bf16[128,1024]{1,0:T(8,128)(2,1)}) %reduce-scatter.42.cloned.1.call-update) | async-done | bytes 262160
  1032.0 20.2 %reduce-scatter.38.cloned.1.call-done = bf16[128,1024]{1,0:T(8,128)(2,1)} async-done(((bf16[512,1024]{1,0:T(8,128)(2,1)}), bf16[128,1024]{1,0:T(8,128)(2,1)}) %reduce-scatter.38.cloned.1.call-update) | async-done | bytes 262160 | tf_op jit(solution)/shard_map/reduce_scatter | solution.py:138
  1052.2 20.6 %reduce-scatter.32.cloned.1.call-done = bf16[128,256]{1,0:T(8,128)(2,1)} async-done(((bf16[512,256]{1,0:T(8,128)(2,1)}), bf16[128,256]{1,0:T(8,128)(2,1)}) %reduce-scatter.32.cloned.1.call-update) | async-done | bytes 65552 | tf_op jit(solution)/shard_map/reduce_scatter | solution.py:126
  1072.8 20.4 %reduce-scatter.36.cloned.1.call-done = bf16[128,256]{1,0:T(8,128)(2,1)} async-done(((bf16[512,256]{1,0:T(8,128)(2,1)}), bf16[128,256]{1,0:T(8,128)(2,1)}) %reduce-scatter.36.cloned.1.call-update) | async-done | bytes 65552 | tf_op jit(solution)/shard_map/reduce_scatter | solution.py:132
  1093.2 20.4 %reduce-scatter.34.cloned.1.call-done = bf16[128,256]{1,0:T(8,128)(2,1)} async-done(((bf16[512,256]{1,0:T(8,128)(2,1)}), bf16[128,256]{1,0:T(8,128)(2,1)}) %reduce-scatter.34.cloned.1.call-update) | async-done | bytes 65552 | tf_op jit(solution)/shard_map/reduce_scatter | solution.py:129
  1134.7 19.2 %reduce-scatter.44.cloned.1.call-done = bf16[16,4]{1,0:T(8,128)(2,1)} async-done(((bf16[64,4]{1,0:T(8,128)(2,1)}), bf16[16,4]{1,0:T(8,128)(2,1)}) %reduce-scatter.44.cloned.1.call-update) | async-done | bytes 144
  1154.6 19.5 %reduce-scatter.46.cloned.1.call-done = bf16[16,4]{1,0:T(8,128)(2,1)} async-done(((bf16[64,4]{1,0:T(8,128)(2,1)}), bf16[16,4]{1,0:T(8,128)(2,1)}) %reduce-scatter.46.cloned.1.call-update) | async-done | bytes 144
  1174.8 50.8 %all-reduce.23.cloned.1.call-done = (bf16[128,256]{1,0:T(8,128)(2,1)}, bf16[128,256]{1,0:T(8,128)(2,1)}, bf16[128,256]{1,0:T(8,128)(2,1)}, bf16[256,128]{1,0:T(8...) async-done(((bf16[128,256]{1,0:T(8,128)(2,1)}, bf16[128,256]{1,0:T(8,128)(2,1)}, bf16[128,256]{1,0:T(8,128)(2,1)}, bf16[256,128]{1,0:T(8,128)(2,1)}, ...) | async-done | bytes 786448 | tf_op jit(solution)/shard_map/psum | solution.py:173
  1234.4 32.8 %all-reduce.17.cloned.1.call-done = (f32[1024,512]{1,0:T(8,128)}, f32[1024,512]{1,0:T(8,128)}, f32[1024,512]{1,0:T(8,128)}, f32[1024,512]{1,0:T(8,128)}) async-done(((f32[1024,512]{1,0:T(8,128)}, f32[1024,512]{1,0:T(8,128)}, f32[1024,512]{1,0:T(8,128)}, f32[1024,512]{1,0:T(8,128)}), (f32[1024,512]{1,0:T(8,128)}, f32[1024,512]{1,0:T(8,128)}, f32[1024,512]{1,0:T(8,128)}, ...) | async-done | bytes 8388624 | tf_op jit(solution)/shard_map/psum | solution.py:192
  (518 shorter events, 642.0 us)
Async XLA Ops:
  8.1 111.8 %all-gather.18.cloned.1.call-start = ((), (), s32[]{:S(2)}) async-start(), calls=%async_computation.14 | async-start | bytes 2621440 | tf_op jit(solution)/shard_map/all_gather | solution.py:351
  10.2 46.4 %copy-start.65 = (f32[1024]{0:T(1024)}, f32[1024]{0:T(1024)S(1)}, u32[]{:S(2)}) copy-start(f32[1024]{0:T(1024)S(1)} %get-tuple-element.550) | copy-start | bytes 12292
  10.2 46.4 %copy-start.67 = (f32[1024]{0:T(1024)}, f32[1024]{0:T(1024)S(1)}, u32[]{:S(2)}) copy-start(f32[1024]{0:T(1024)S(1)} %get-tuple-element.551) | copy-start | bytes 12292
  58.9 71.2 %all-gather.16.cloned.1.call-start = ((), (), s32[]{:S(2)}) async-start(), calls=%async_computation.13 | async-start | bytes 2621440 | tf_op jit(solution)/shard_map/all_gather | solution.py:350
  75.6 144.0 %all-gather.26.cloned.1.call-start = ((), (), s32[]{:S(2)}) async-start(), calls=%async_computation.18 | async-start | bytes 2621440 | tf_op jit(solution)/shard_map/all_gather | solution.py:351
  76.9 146.8 %all-gather.24.cloned.1.call-start = ((), (), s32[]{:S(2)}) async-start(), calls=%async_computation.17 | async-start | bytes 2621440 | tf_op jit(solution)/shard_map/all_gather | solution.py:350
  78.3 276.1 %all-reduce.21.cloned.1.call-start = ((), (), s32[]{:S(2)}) async-start(), calls=%async_computation.34 | async-start | bytes 8388608 | tf_op jit(solution)/shard_map/psum | solution.py:192
  316.6 42.8 %all-gather.20.cloned.1.call-start = ((), (), s32[]{:S(2)}) async-start(), calls=%async_computation.15 | async-start | bytes 1310720 | tf_op jit(solution)/shard_map/all_gather | solution.py:77
  317.1 69.2 %all-gather.22.cloned.1.call-start = ((), (), s32[]{:S(2)}) async-start(), calls=%async_computation.16 | async-start | bytes 1310720 | tf_op jit(solution)/shard_map/all_gather | solution.py:78
  317.7 115.2 %all-reduce.19.cloned.1.call-start = ((), (), s32[]{:S(2)}) async-start(), calls=%async_computation.33 | async-start | bytes 8388608 | tf_op jit(solution)/shard_map/psum | solution.py:196
  336.4 101.4 %copy-start.88 = (f32[4,1,128]{2,1,0:T(1,128)}, f32[4,1,128]{2,1,0:T(1,128)S(1)}, u32[]{:S(2)}) copy-start(f32[4,1,128]{2,1,0:T(1,128)S(1)} %convert_element_type.453) | copy-start | bytes 6148
  357.4 80.5 %copy-start.71 = (f32[1024]{0:T(1024)}, f32[1024]{0:T(1024)S(1)}, u32[]{:S(2)}) copy-start(f32[1024]{0:T(1024)S(1)} %broadcast_multiply_fusion.10) | copy-start | bytes 12292
  357.8 80.1 %copy-start.82 = (f32[1024]{0:T(1024)}, f32[1024]{0:T(1024)S(1)}, u32[]{:S(2)}) copy-start(f32[1024]{0:T(1024)S(1)} %add_rsqrt_fusion.2) | copy-start | bytes 12292
  357.8 80.1 %copy-start.69 = (f32[1024]{0:T(1024)}, f32[1024]{0:T(1024)S(1)}, u32[]{:S(2)}) copy-start(f32[1024]{0:T(1024)S(1)} %broadcast_multiply_fusion.8) | copy-start | bytes 12292
  359.3 78.5 %copy-start.84 = (f32[1024]{0:T(1024)}, f32[1024]{0:T(1024)S(1)}, u32[]{:S(2)}) copy-start(f32[1024]{0:T(1024)S(1)} %add_rsqrt_fusion) | copy-start | bytes 12292
  405.7 486.9 %reduce-scatter.26.cloned.1.call-start = ((), (), s32[]{:S(2)}) async-start(), calls=%async_computation.20 | async-start | bytes 2621440 | tf_op jit(solution)/shard_map/reduce_scatter | solution.py:391
  650.0 247.3 %reduce-scatter.30.cloned.1.call-start = ((), (), s32[]{:S(2)}) async-start(), calls=%async_computation.22 | async-start | bytes 2621440 | tf_op jit(solution)/shard_map/reduce_scatter | solution.py:391
  860.9 74.6 %reduce-scatter.24.cloned.1.call-start = ((), (), s32[]{:S(2)}) async-start(), calls=%async_computation.19 | async-start | bytes 2621440 | tf_op jit(solution)/shard_map/reduce_scatter | solution.py:388
  864.8 109.3 %reduce-scatter.28.cloned.1.call-start = ((), (), s32[]{:S(2)}) async-start(), calls=%async_computation.21 | async-start | bytes 2621440 | tf_op jit(solution)/shard_map/reduce_scatter | solution.py:388
  868.7 135.1 %reduce-scatter.42.cloned.1.call-start = ((), (), s32[]{:S(2)}) async-start(), calls=%async_computation.28 | async-start | bytes 1310720
  878.0 146.4 %reduce-scatter.40.cloned.1.call-start = ((), (), s32[]{:S(2)}) async-start(), calls=%async_computation.27 | async-start | bytes 327680
  882.1 170.1 %reduce-scatter.38.cloned.1.call-start = ((), (), s32[]{:S(2)}) async-start(), calls=%async_computation.26 | async-start | bytes 1310720 | tf_op jit(solution)/shard_map/reduce_scatter | solution.py:138
  888.0 184.8 %reduce-scatter.32.cloned.1.call-start = ((), (), s32[]{:S(2)}) async-start(), calls=%async_computation.23 | async-start | bytes 327680 | tf_op jit(solution)/shard_map/reduce_scatter | solution.py:126
  892.5 200.7 %reduce-scatter.36.cloned.1.call-start = ((), (), s32[]{:S(2)}) async-start(), calls=%async_computation.25 | async-start | bytes 327680 | tf_op jit(solution)/shard_map/reduce_scatter | solution.py:132
  899.7 76.9 %copy-start.100 = (f32[1024]{0:T(1024)S(1)}, f32[1024]{0:T(1024)}, u32[]{:S(2)}) copy-start(f32[1024]{0:T(1024)} %get-tuple-element.546) | copy-start | bytes 12292
  899.7 76.9 %copy-start.101 = (f32[1024]{0:T(1024)S(1)}, f32[1024]{0:T(1024)}, u32[]{:S(2)}) copy-start(f32[1024]{0:T(1024)} %get-tuple-element.548) | copy-start | bytes 12292
  899.7 213.8 %reduce-scatter.34.cloned.1.call-start = ((), (), s32[]{:S(2)}) async-start(), calls=%async_computation.24 | async-start | bytes 327680 | tf_op jit(solution)/shard_map/reduce_scatter | solution.py:129
  976.5 157.3 %reduce-scatter.48.cloned.1.call-start = ((), (), s32[]{:S(2)}) async-start(), calls=%async_computation.31 | async-start | bytes 81920
  977.4 176.5 %reduce-scatter.44.cloned.1.call-start = ((), (), s32[]{:S(2)}) async-start(), calls=%async_computation.29 | async-start | bytes 20480
  1011.5 162.6 %reduce-scatter.46.cloned.1.call-start = ((), (), s32[]{:S(2)}) async-start(), calls=%async_computation.30 | async-start | bytes 20480
  1027.1 198.5 %all-reduce.23.cloned.1.call-start = ((), (), s32[]{:S(2)}) async-start(), calls=%async_computation.35 | async-start | bytes 1572864 | tf_op jit(solution)/shard_map/psum | solution.py:173
  1113.6 153.6 %all-reduce.17.cloned.1.call-start = ((), (), s32[]{:S(2)}) async-start(), calls=%async_computation.32 | async-start | bytes 16777216 | tf_op jit(solution)/shard_map/psum | solution.py:192
  (120 other events, 1070.5 us)
Sparse Core Ops, SparseCore 0:
  59.0 33.3 all-gather.17
  94.8 35.1 all-gather.15
  132.5 35.1 all-gather.25
  170.0 35.1 all-gather.23
  316.7 28.5 all-reduce.20
  405.8 27.0 all-reduce.18
  650.1 36.3 reduce-scatter.25
  861.0 36.2 reduce-scatter.29
  900.3 35.1 reduce-scatter.23
  938.9 35.1 reduce-scatter.27
  976.4 27.2 reduce-scatter.41
  1005.8 18.4 reduce-scatter.39
  1026.7 25.5 reduce-scatter.37
  1054.3 18.4 reduce-scatter.31
  1074.9 18.2 reduce-scatter.35
  1095.3 18.2 reduce-scatter.33
  1116.2 17.5 reduce-scatter.47
  1136.5 17.3 reduce-scatter.43
  1156.7 17.3 reduce-scatter.45
  1178.2 47.3 all-reduce.22
  1229.0 38.1 all-reduce.16
Sparse Core Ops, SparseCore 1:
  318.6 28.2 all-gather.19
  348.3 29.0 all-gather.21
where the time goes:
time: 1320 us
  matrix products  497 us (38%)
  waiting for transfers between devices  348 us (26%)
  other arithmetic  226 us (17%)
  blocking collectives  160 us (12%)
  local copies, waits for them, and re-layouts  65.7 us (5%)
  between operations  18.4 us (1%)
    convert_element_type x4, other arithmetic, one_block(): grad_scores = (prob_rows * (grad_probs - row_delta)).astype(jnp.bfloat16)  110 us
    dot_general x8, matrix products, one_block(): jnp.einsum('qhd,khd->hqk', query_block, key_heads, preferred_element_type...  106 us
    dot_general x4, matrix products, one_block(): jnp.einsum('qhd,khd->hqk', grad_block, value_heads, preferred_element_typ...  91.9 us
    unnamed x28, waiting for transfers between devices  75.7 us
    reduce_scatter x2, waiting for transfers between devices, body(): lax.psum_scatter(grad_keys_all.astype(jnp.bfloat16), 'ctx', scatter_dimen...  71.7 us
    dot_general x4, matrix products, one_block(): jnp.einsum('hqk,qhd->khd', prob_rows.astype(jnp.bfloat16), grad_block, pr...  66 us
    dot_general x4, matrix products, one_block(): jnp.einsum('hqk,khd->qhd', attn_weights, value_heads, preferred_element_t...  59.1 us
    reduce_sum x4, other arithmetic, one_block(): row_total = jnp.sum(exponent, axis=-1, keepdims=True)  56.4 us
  transfers between devices with their start and end apart: 23, of which 16 were waited for; matrix products, arithmetic and copies ran while one was open for 32% of the time, Pallas kernels for 0%

commit v1 on v0

v1 whole, which is shorter than its diff:
```python
import functools
import math

import jax
import jax.numpy as jnp
from jax import lax
from jax.experimental import pallas as pl
from jax.experimental.pallas import tpu as pltpu
from jax.sharding import PartitionSpec as P

F32 = jnp.float32
BF16 = jnp.bfloat16
MESH = pl.DeviceIdType.MESH
norm_eps = 1e-05
LOG2E = math.log2(math.e)
VMEM_LIMIT = 60 * 2**20


def dot_nn(left, right):
    return lax.dot_general(left, right, (((1,), (0,)), ((), ())), preferred_element_type=F32)


def dot_nt(left, right):
    return lax.dot_general(left, right, (((1,), (1,)), ((), ())), preferred_element_type=F32)


def dot_tn(left, right):
    return lax.dot_general(left, right, (((0,), (0,)), ((), ())), preferred_element_type=F32)


def unit_norm(values):
    average = jnp.mean(values, axis=-1, keepdims=True)
    centred = values - average
    variance = jnp.mean(centred * centred, axis=-1, keepdims=True)
    inverse = lax.rsqrt(variance + norm_eps)
    return centred * inverse, inverse


def norm_back(grad_normed, unit_vals, inverse, gain):
    scaled = grad_normed * gain
    return inverse * (
        scaled
        - jnp.mean(scaled, axis=-1, keepdims=True)
        - unit_vals * jnp.mean(scaled * unit_vals, axis=-1, keepdims=True)
    )


def column_sum(values):
    return jnp.sum(values, axis=0, keepdims=True)


def full_spec(shape):
    return pl.BlockSpec(shape, lambda *_: (0,) * len(shape))


def params(limit=VMEM_LIMIT, **others):
    return pltpu.CompilerParams(vmem_limit_bytes=limit, **others)


def gather_kernel(ns, nc, w_ref, small_ref, x_ref, w_out, small_out, x_out, *sems):
    w_send, w_recv, s_send, s_recv, x_send, x_recv, wt_send, wt_recv, st_send, st_recv, xt_send, xt_recv, local = sems
    s = lax.axis_index("shard")
    c = lax.axis_index("ctx")
    t = lax.axis_index("tp")
    other = 1 - t
    depth = w_ref.shape[1]
    half = x_ref.shape[0] // 2

    barrier = pltpu.get_barrier_semaphore()
    for d in range(1, ns):
        pl.semaphore_signal(barrier, inc=1, device_id={"shard": s ^ d}, device_id_type=MESH)
    for d in range(1, nc):
        pl.semaphore_signal(barrier, inc=1, device_id={"ctx": c ^ d}, device_id_type=MESH)
    pl.semaphore_signal(barrier, inc=1, device_id={"tp": other}, device_id_type=MESH)
    pl.semaphore_wait(barrier, ns + nc - 1)

    def w_rows(part, owner):
        return w_out.at[part, :, pl.ds(pl.multiple_of(owner * depth, depth), depth), :]

    def x_rows(which):
        return x_ref.at[pl.ds(pl.multiple_of(which * half, half), half), :]

    def send(source, target, send_sem, recv_sem, where):
        copy = pltpu.make_async_remote_copy(
            src_ref=source, dst_ref=target, send_sem=send_sem, recv_sem=recv_sem,
            device_id=where, device_id_type=MESH,
        )
        copy.start()
        return copy

    sent = []
    x_copies, w_copies, s_copies = {}, {}, {}
    for d in range(1, nc):
        x_copies[d] = send(x_rows(t), x_out.at[d, 0], x_send.at[d], x_recv.at[d], {"ctx": c ^ d})
    for d in range(1, ns):
        w_copies[d] = send(w_ref, w_rows(0, s), w_send.at[d], w_recv.at[d], {"shard": s ^ d})
        s_copies[d] = send(small_ref, small_out.at[0, s], s_send.at[d], s_recv.at[d], {"shard": s ^ d})
    last = [
        send(w_ref, w_rows(1, s), wt_send.at[0], wt_recv.at[0], {"tp": other}),
        send(small_ref, small_out.at[1, s], st_send.at[0], st_recv.at[0], {"tp": other}),
    ]
    locals_ = [
        pltpu.make_async_copy(w_ref, w_rows(0, s), local.at[0]),
        pltpu.make_async_copy(small_ref, small_out.at[0, s], local.at[1]),
        pltpu.make_async_copy(x_rows(t), x_out.at[0, 0], local.at[2]),
        pltpu.make_async_copy(x_rows(other), x_out.at[0, 1], local.at[3]),
    ]
    for copy in locals_:
        copy.start()
    for d in range(1, max(ns, nc)):
        if d < ns:
            w_copies[d].wait_recv()
            last.append(send(w_rows(0, s ^ d), w_rows(1, s ^ d), wt_send.at[d], wt_recv.at[d], {"tp": other}))
            s_copies[d].wait_recv()
            last.append(
                send(small_out.at[0, s ^ d], small_out.at[1, s ^ d], st_send.at[d], st_recv.at[d], {"tp": other})
            )
        if d < nc:
            x_copies[d].wait_recv()
            last.append(send(x_out.at[d, 0], x_out.at[d, 1], xt_send.at[d], xt_recv.at[d], {"tp": other}))
    for copies in (x_copies, w_copies, s_copies):
        for copy in copies.values():
            copy.wait_send()
    for copy in last:
        copy.wait()
    for copy in locals_:
        copy.wait()


def gather_first(w_stack, small, x_rows, ns, nc):
    kinds, depth, width = w_stack.shape
    length, features = x_rows.shape
    dma = pltpu.SemaphoreType.DMA
    return pl.pallas_call(
        functools.partial(gather_kernel, ns, nc),
        in_specs=[pl.BlockSpec(memory_space=pltpu.VMEM)] * 3,
        out_specs=[pl.BlockSpec(memory_space=pl.ANY)] * 3,
        out_shape=[
            jax.ShapeDtypeStruct((2, kinds, ns * depth, width), BF16),
            jax.ShapeDtypeStruct((2, ns) + small.shape, BF16),
            jax.ShapeDtypeStruct((nc, 2, length // 2, features), BF16),
        ],
        scratch_shapes=[dma((ns,)), dma((ns,)), dma((ns,)), dma((ns,)), dma((nc,)), dma((nc,))]
        + [dma((ns,)), dma((ns,)), dma((ns,)), dma((ns,)), dma((nc,)), dma((nc,)), dma((4,))],
        compiler_params=params(collective_id=0, has_side_effects=True),
        name="gather_first",
    )(w_stack, small, x_rows)


def front_kernel(x_ref, w_ref, gain_ref, shift_ref, bq_ref, bv_ref, n_ref, k_ref, v_ref, q_ref, *, q_scale):
    step = pl.program_id(0)
    unit, _ = unit_norm(x_ref[...].astype(F32))
    normed = (unit * gain_ref[...] + shift_ref[...]).astype(BF16)
    n_ref[...] = normed
    width = w_ref.shape[3]
    for part in range(2):
        cols = slice(part * width, (part + 1) * width)
        k_ref[:, cols] = dot_nn(normed, w_ref[part, 1]).astype(BF16)
        v_ref[:, cols] = (dot_nn(normed, w_ref[part, 2]) + bv_ref[:, cols]).astype(BF16)

    @pl.when(step == 0)
    def _():
        for part in range(2):
            cols = slice(part * width, (part + 1) * width)
            q_ref[:, cols] = ((dot_nn(normed, w_ref[part, 0]) + bq_ref[:, cols]) * q_scale).astype(BF16)


def front(x_all, weights, gain, shift, b_query, b_value, head_width):
    keys, features = x_all.shape
    block = keys // 8
    width = 2 * weights.shape[3]
    return pl.pallas_call(
        functools.partial(front_kernel, q_scale=LOG2E / math.sqrt(head_width)),
        grid=(8,),
        in_specs=[
            pl.BlockSpec((block, features), lambda i: (i, 0)),
            full_spec(weights.shape),
            full_spec((1, features)),
            full_spec((1, features)),
            full_spec((1, width)),
            full_spec((1, width)),
        ],
        out_specs=[
            pl.BlockSpec((block, features), lambda i: (i, 0)),
            pl.BlockSpec((block, width), lambda i: (i, 0)),
            pl.BlockSpec((block, width), lambda i: (i, 0)),
            full_spec((block, width)),
        ],
        out_shape=[
            jax.ShapeDtypeStruct((keys, features), BF16),
            jax.ShapeDtypeStruct((keys, width), BF16),
            jax.ShapeDtypeStruct((keys, width), BF16),
            jax.ShapeDtypeStruct((block, width), BF16),
        ],
        compiler_params=params(),
        cost_estimate=pl.CostEstimate(
            flops=4 * keys * features * width, bytes_accessed=8 * keys * features, transcendentals=keys
        ),
        name="front",
    )(x_all, weights, gain, shift, b_query, b_value)


def with_parts(lane, base, values, first, width):
    high = values.astype(BF16).astype(F32)
    rest = values - high
    middle = rest.astype(BF16).astype(F32)
    low = rest - middle
    extra = jnp.where(
        lane == first, high, jnp.where(lane == first + 1, middle, jnp.where(lane == first + 2, low, 0.0))
    )
    inside = (lane < width) if first else (lane >= width)
    return jnp.where(inside, base, extra)


def send(source, target, send_sem, recv_sem, where):
    return pltpu.make_async_remote_copy(
        src_ref=source, dst_ref=target, send_sem=send_sem, recv_sem=recv_sem, device_id=where, device_id_type=MESH
    )


def greet(counts):
    barrier = pltpu.get_barrier_semaphore()
    total = 0
    for name, count in counts:
        me = lax.axis_index(name)
        for d in range(1, count):
            pl.semaphore_signal(barrier, inc=1, device_id={name: me ^ d}, device_id_type=MESH)
            total += 1
    pl.semaphore_wait(barrier, total)


class Gather:

    def __init__(self, name, count, source, theirs, target, place, sems):
        self.name, self.count, self.source, self.theirs = name, count, source, theirs
        self.target, self.place = target, place
        self.out_sem, self.in_sem, self.cross_out, self.cross_in, self.local = sems
        self.me = lax.axis_index(name)

    def first(self, d):
        where = {self.name: self.me ^ d}
        return send(self.source, self.place(self.target, 0, self.me, d), self.out_sem.at[d], self.in_sem.at[d], where)

    def cross(self, d):
        where = {"tp": 1 - lax.axis_index("tp")}
        owner = self.me ^ d
        source = self.place(self.target, 0, owner, d) if d else self.source
        return send(source, self.place(self.target, 1, owner, d), self.cross_out.at[d], self.cross_in.at[d], where)

    def locals(self):
        copies = [pltpu.make_async_copy(self.source, self.place(self.target, 0, self.me, 0), self.local.at[0])]
        if self.theirs is not None:
            copies.append(pltpu.make_async_copy(self.theirs, self.place(self.target, 1, self.me, 0), self.local.at[1]))
        return copies

    def crossed(self):
        return range(0 if self.theirs is None else 1, self.count)

    def start(self):
        for d in range(1, self.count):
            self.first(d).start()
        for copy in self.locals():
            copy.start()
        if self.theirs is None:
            self.cross(0).start()

    def forward(self):
        for d in range(1, self.count):
            self.first(d).wait_recv()
            self.cross(d).start()

    def finish(self):
        for d in range(1, self.count):
            self.first(d).wait_send()
        for d in self.crossed():
            self.cross(d).wait()
        for copy in self.locals():
            copy.wait()


def place_rows(ref, part, owner, d):
    size = ref.shape[1] // lax.axis_size("shard")
    return ref.at[part, pl.ds(pl.multiple_of(owner * size, size), size), :]


def place_columns(ref, part, owner, d):
    size = ref.shape[2] // lax.axis_size("shard")
    return ref.at[part, :, pl.ds(pl.multiple_of(owner * size, size), size)]


def place_slot(ref, part, owner, d):
    return ref.at[part, owner]


def place_distance(ref, part, owner, d):
    return ref.at[d, part]


def gather_sems(count):
    dma = pltpu.SemaphoreType.DMA
    return [dma((count,)), dma((count,)), dma((count,)), dma((count,)), dma((2,))]


def attend_kernel(*refs, kc, width, plans):
    count = len(plans)
    q_ref, k_ref, v_ref = refs[:3]
    sources = refs[3 : 3 + count]
    o_ref, qx_ref = refs[3 + count : 5 + count]
    targets = refs[5 + count : 5 + 2 * count]
    scores = refs[5 + 2 * count]
    sems = refs[6 + 2 * count :]
    step = pl.program_id(0)
    last = pl.num_programs(0) - 1
    t = lax.axis_index("tp")

    def gathers(wanted):
        found = []
        for i, (name, number, place, split) in enumerate(plans):
            if name != wanted:
                continue
            source, theirs = sources[i], None
            if split:
                half = source.shape[0] // 2
                theirs = source.at[pl.ds(pl.multiple_of((1 - t) * half, half), half), :]
                source = source.at[pl.ds(pl.multiple_of(t * half, half), half), :]
            found.append(Gather(name, number, source, theirs, targets[i], place, sems[5 * i : 5 * i + 5]))
        return found

    counts = {name: number for name, number, _, _ in plans}

    @pl.when(step == 0)
    def _():
        greet([("tp", 2)] + list(counts.items()))
        for name in counts:
            for gather in gathers(name):
                gather.start()

    @pl.when(step == last)
    def _():
        for gather in gathers("ctx"):
            gather.forward()

    rows, lanes = q_ref.shape
    keys = k_ref.shape[0]
    lane = lax.broadcasted_iota(jnp.int32, (rows, lanes), 1)
    lane_v = lax.broadcasted_iota(jnp.int32, (kc, lanes), 1)
    q = q_ref[...].astype(F32)
    tops = []
    for h in range(2):
        inside = (lane < width) if h == 0 else (lane >= width)
        q_head = jnp.where(inside, q, 0.0).astype(BF16)
        top = None
        for i in range(keys // kc):
            part = dot_nt(k_ref[i * kc : (i + 1) * kc], q_head)
            scores[h, i * kc : (i + 1) * kc] = part
            here = jnp.max(part.reshape(kc // 8, 8, rows), axis=0)
            top = here if top is None else jnp.maximum(top, here)
        tops.append(jnp.max(top, axis=0, keepdims=True))
    outs = []
    for h in range(2):
        inside_v = (lane_v < width) if h == 0 else (lane_v >= width)
        total = jnp.zeros((lanes, rows), F32)
        for i in range(keys // kc):
            v_one = jnp.where(inside_v, v_ref[i * kc : (i + 1) * kc], jnp.ones((), BF16))
            exponent = jnp.exp2(scores[h, i * kc : (i + 1) * kc] - tops[h]).astype(BF16)
            total += dot_tn(v_one, exponent)
        first = width if h == 0 else 0
        log_total = tops[h] + jnp.log2(total[first : first + 1, :])
        total = total.T
        outs.append(total / pltpu.roll(total, width, 1))
        log_column = jnp.broadcast_to(log_total, (8, rows)).T[:, :1]
        qx_ref[:, h * lanes : (h + 1) * lanes] = with_parts(lane, q, -log_column, first, width).astype(BF16)
    o_ref[...] = jnp.where(lane < width, outs[0], outs[1]).astype(BF16)

    @pl.when(step == last)
    def _():
        for gather in gathers("shard"):
            gather.forward()
        for name in counts:
            for gather in gathers(name):
                gather.finish()


def attend_forward(q, k, v, width, plans, sources, shapes, number):
    rows, cols = q.shape
    keys = k.shape[0]
    lanes = 2 * width
    kc = 512
    anywhere = pl.BlockSpec(memory_space=pl.ANY)
    return pl.pallas_call(
        functools.partial(attend_kernel, kc=kc, width=width, plans=plans),
        grid=(cols // lanes,),
        in_specs=[
            pl.BlockSpec((rows, lanes), lambda j: (0, j)),
            pl.BlockSpec((keys, lanes), lambda j: (0, j)),
            pl.BlockSpec((keys, lanes), lambda j: (0, j)),
        ]
        + [anywhere] * len(plans),
        out_specs=[
            pl.BlockSpec((rows, lanes), lambda j: (0, j)),
            pl.BlockSpec((rows, 2 * lanes), lambda j: (0, j)),
        ]
        + [anywhere] * len(plans),
        out_shape=[
            jax.ShapeDtypeStruct((rows, cols), BF16),
            jax.ShapeDtypeStruct((rows, 2 * cols), BF16),
        ]
        + [jax.ShapeDtypeStruct(shape, BF16) for shape in shapes],
        scratch_shapes=[pltpu.VMEM((2, keys, rows), F32)]
        + [sem for plan in plans for sem in gather_sems(plan[1])],
        compiler_params=params(collective_id=number, has_side_effects=True),
        cost_estimate=pl.CostEstimate(
            flops=12 * rows * keys * cols, bytes_accessed=4 * keys * cols, transcendentals=rows * keys * cols // width
        ),
        name="attend_forward",
    )(q, k, v, *sources)


def attend_back_step(qx_ref, k_ref, v_ref, go_ref, o_ref, dq_ref, dk_ref, dv_ref, width):
    rows, lanes = o_ref.shape
    keys = k_ref.shape[0]
    lane = lax.broadcasted_iota(jnp.int32, (rows, lanes), 1)
    lane_k = lax.broadcasted_iota(jnp.int32, (keys, lanes), 1)
    one = jnp.ones((), BF16)
    grad_out = go_ref[...].astype(F32)
    both = grad_out * o_ref[...].astype(F32)
    grad_k, grad_v, grad_q = [], [], []
    for h in range(2):
        inside = (lane < width) if h == 0 else (lane >= width)
        inside_k = (lane_k < width) if h == 0 else (lane_k >= width)
        first = width if h == 0 else 0
        delta = jnp.sum(jnp.where(inside, both, 0.0), axis=1, keepdims=True)
        gx = with_parts(lane, grad_out, -delta, first, width).astype(BF16)
        kx = jnp.where(inside_k, k_ref[...], one)
        vx = jnp.where(inside_k, v_ref[...], one)
        qx = qx_ref[:, h * lanes : (h + 1) * lanes]
        prob = jnp.exp2(dot_nt(kx, qx))
        grad_v.append(dot_nn(prob.astype(BF16), gx))
        grad_score = (prob * dot_nt(vx, gx)).astype(BF16)
        grad_k.append(dot_nn(grad_score, qx))
        grad_q.append(dot_tn(kx, grad_score))
    dk_ref[...] = (jnp.where(lane_k < width, grad_k[0], grad_k[1]) * (1.0 / LOG2E)).astype(BF16)
    dv_ref[...] = jnp.where(lane_k < width, grad_v[0], grad_v[1]).astype(BF16)
    grad_both = jnp.concatenate([grad_q[0][:width], grad_q[1][width:]], axis=0)
    dq_ref[...] = (grad_both.T * (1.0 / math.sqrt(width))).astype(BF16)


def sum_rows(target, at, left, left_at, right, right_at, rows, chunk=64):
    def one(i, carry):
        here = pl.multiple_of(i * chunk, chunk)
        value = left[pl.ds(left_at + here, chunk), :].astype(F32) + right[pl.ds(right_at + here, chunk), :].astype(F32)
        target[pl.ds(at + here, chunk), :] = value.astype(target.dtype)
        return carry

    lax.fori_loop(0, rows // chunk, one, 0)


class Axis:

    def __init__(self, name, count, sems):
        self.name, self.count, self.sems = name, count, sems
        self.me = lax.axis_index(name)

    def copy(self, d, source, target):
        return send(source(self.me ^ d, d), target(self.me, d), self.sems[0].at[d], self.sems[1].at[d], {self.name: self.me ^ d})

    def start(self, source, target):
        for d in range(1, self.count):
            self.copy(d, source, target).start()

    def wait(self, source, target):
        for d in range(1, self.count):
            self.copy(d, source, target).wait()


def axis_sems(*counts):
    return [pltpu.SemaphoreType.DMA((count,)) for count in counts for _ in range(2)]


def cross(source, target, sems, i):
    return send(source, target, sems[0].at[i], sems[1].at[i], {"tp": 1 - lax.axis_index("tp")})


class RowSum:

    def __init__(self, dw_send, dw_own, extra, received, total, blocks, tp_sems, ctx):
        self.dw_send, self.dw_own, self.extra = dw_send, dw_own, extra
        self.received, self.total, self.blocks = received, total, blocks
        self.tp_sems, self.ctx = tp_sems, ctx
        self.main, self.more = dw_own.shape[0], extra.shape[1]
        self.size = (self.main + self.more) // ctx.count

    def crossing(self):
        return [
            cross(self.dw_send, self.received.at[pl.ds(0, self.main), :], self.tp_sems, 0),
            cross(self.extra.at[1], self.received.at[pl.ds(self.main, self.more), :], self.tp_sems, 1),
        ]

    def start(self):
        for copy in self.crossing():
            copy.start()

    def source(self, peer, d):
        return self.total.at[pl.ds(pl.multiple_of(peer * self.size, 16), self.size), :]

    def target(self, me, d):
        return self.blocks.at[d]

    def spread(self):
        for copy in self.crossing():
            copy.wait()
        sum_rows(self.total, 0, self.dw_own, 0, self.received, 0, self.main)
        sum_rows(self.total, self.main, self.extra.at[0], 0, self.received, self.main, self.more)
        self.ctx.start(self.source, self.target)

    def finish(self, out):
        self.ctx.wait(self.source, self.target)
        count, size, width = out.shape
        value = self.total[pl.ds(pl.multiple_of(self.ctx.me * self.size, 16), self.size), :].astype(F32)
        for d in range(1, self.ctx.count):
            value += self.blocks[d].astype(F32)
        for j in range(count):
            out[j] = value[:, j * width : (j + 1) * width].astype(out.dtype)


class ShardSum:

    def __init__(self, parts, received, blocks, shard, ctx):
        self.parts, self.received, self.blocks, self.shard, self.ctx = parts, received, blocks, shard, ctx

    def source(self, peer, d):
        return self.parts.at[peer]

    def target(self, me, d):
        return self.received.at[d]

    def start(self):
        self.shard.start(self.source, self.target)

    def mine(self, peer, d):
        return self.blocks.at[self.ctx.me]

    def theirs(self, me, d):
        return self.blocks.at[me]

    def spread(self):
        self.shard.wait(self.source, self.target)
        value = self.parts[self.shard.me].astype(F32)
        for d in range(1, self.shard.count):
            value += self.received[d].astype(F32)
        self.blocks[self.ctx.me] = value.astype(BF16)
        self.ctx.start(self.mine, self.theirs)

    def finish(self):
        self.ctx.wait(self.mine, self.theirs)


class InputSum:

    def __init__(self, dn_send, dn_own, received, total, blocks, tp_sems, ctx):
        self.dn_send, self.dn_own, self.received = dn_send, dn_own, received
        self.total, self.blocks, self.tp_sems, self.ctx = total, blocks, tp_sems, ctx

    def crossing(self, d):
        return cross(self.dn_send(d), self.received.at[d], self.tp_sems, d)

    def start(self):
        for d in reversed(range(self.ctx.count)):
            self.crossing(d).start()

    def source(self, peer, d):
        return self.total.at[d]

    def target(self, me, d):
        return self.blocks.at[d]

    def spread(self):
        for d in reversed(range(self.ctx.count)):
            self.crossing(d).wait()
            rows = self.received.shape[1]
            sum_rows(self.total.at[d], 0, self.dn_own(d), 0, self.received.at[d], 0, rows)
            if d:
                self.ctx.copy(d, self.source, self.target).start()

    def finish(self):
        self.ctx.wait(self.source, self.target)

    def rows(self, at, size):
        value = self.total[0, pl.ds(at, size), :].astype(F32)
        for d in range(1, self.ctx.count):
            value += self.blocks[d, pl.ds(at, size), :].astype(F32)
        return value


def attend_back_one(
    qx_ref, k_ref, v_ref, go_ref, o_ref, dw_all, dw_own, extra, out_half,
    dq_ref, dk_ref, dv_ref, dw_out, whole,
    received, total, blocks, tp_out, tp_in, ctx_out, ctx_in, whole_sems, *, width, nc,
):
    step = pl.program_id(0)
    last = pl.num_programs(0) - 1
    t = lax.axis_index("tp")
    rows = RowSum(dw_all.at[1], dw_own.at[0], extra, received, total, blocks, (tp_out, tp_in), Axis("ctx", nc, (ctx_out, ctx_in)))

    def whole_copies():
        return [
            cross(out_half, whole.at[:, t], (whole_sems, whole_sems.at[pl.ds(1, 1)]), 0),
            pltpu.make_async_copy(out_half, whole.at[:, t], whole_sems.at[2]),
        ]

    @pl.when(step == 0)
    def _():
        greet([("tp", 2), ("ctx", nc)])
        rows.start()
        for copy in whole_copies():
            copy.start()

    @pl.when(step == 1)
    def _():
        rows.spread()

    attend_back_step(qx_ref, k_ref, v_ref, go_ref, o_ref, dq_ref, dk_ref, dv_ref, width)

    @pl.when(step == last)
    def _():
        rows.finish(dw_out)
        for copy in whole_copies():
            copy.wait()


def attend_back_two(
    qx_ref, k_ref, v_ref, go_ref, o_ref, dw_parts, dn_all, dn_own,
    dq_ref, dk_ref, dv_ref, dw_done, dn_done,
    dw_received, dw_blocks, dn_received, dn_total, dn_blocks,
    z_out, z_in, back_out, back_in, tp_out, tp_in, ctx_out, ctx_in, *, width, nc, ns,
):
    step = pl.program_id(0)
    last = pl.num_programs(0) - 1
    weights = ShardSum(
        dw_parts, dw_received, dw_blocks, Axis("shard", ns, (z_out, z_in)), Axis("ctx", nc, (back_out, back_in))
    )
    inputs = InputSum(
        lambda d: dn_all.at[d, 1], lambda d: dn_own.at[d, 0], dn_received, dn_total, dn_blocks,
        (tp_out, tp_in), Axis("ctx", nc, (ctx_out, ctx_in)),
    )

    @pl.when(step == 0)
    def _():
        greet([("tp", 2), ("ctx", nc), ("shard", ns)])
        inputs.start()
        weights.start()

    @pl.when(step == 1)
    def _():
        inputs.spread()

    @pl.when(step == 2)
    def _():
        weights.spread()

    attend_back_step(qx_ref, k_ref, v_ref, go_ref, o_ref, dq_ref, dk_ref, dv_ref, width)

    @pl.when(step == last)
    def _():
        inputs.finish()
        weights.finish()
        dw_done[...] = dw_blocks[...]
        size = 64

        def one(i, carry):
            at = pl.multiple_of(i * size, size)
            dn_done[pl.ds(at, size), :] = inputs.rows(at, size)
            return carry

        lax.fori_loop(0, dn_done.shape[0] // size, one, 0)


def attend_back(kernel, qx, k, v, grad_mixed, mixed, width, micro, others, other_specs, out_shapes, out_specs, scratch, number):
    rows, cols = mixed.shape
    keys = k.shape[0]
    lanes = 2 * width
    return pl.pallas_call(
        functools.partial(kernel, width=width),
        grid=(cols // lanes,),
        in_specs=[
            pl.BlockSpec((rows, 2 * lanes), lambda j: (0, j)),
            pl.BlockSpec((keys, lanes), lambda j: (0, j)),
            pl.BlockSpec((keys, lanes), lambda j: (0, j)),
            pl.BlockSpec((rows, lanes), lambda j: (micro, j)),
            pl.BlockSpec((rows, lanes), lambda j: (0, j)),
        ]
        + other_specs,
        out_specs=[
            pl.BlockSpec((rows, lanes), lambda j: (0, j)),
            pl.BlockSpec((keys, lanes), lambda j: (0, j)),
            pl.BlockSpec((keys, lanes), lambda j: (0, j)),
        ]
        + out_specs,
        out_shape=[
            jax.ShapeDtypeStruct((rows, cols), BF16),
            jax.ShapeDtypeStruct((keys, cols), BF16),
            jax.ShapeDtypeStruct((keys, cols), BF16),
        ]
        + out_shapes,
        scratch_shapes=scratch,
        compiler_params=params(collective_id=number, has_side_effects=True),
        cost_estimate=pl.CostEstimate(
            flops=30 * rows * keys * cols, bytes_accessed=8 * keys * cols, transcendentals=rows * keys * cols // width
        ),
        name="attend_back",
    )(qx, k, v, grad_mixed, mixed, *others)


def once(shape, index=None):
    place = index or (0,) * len(shape)
    return pl.BlockSpec(shape, lambda *_: place, pipeline_mode=pl.Buffered(1))


def attend_back_rows(qx, k, v, grad_mixed, mixed, width, micro, dw, extra, out, ns, nc):
    main, features = dw.shape[1:]
    rows = main + extra.shape[1]
    anywhere = pl.BlockSpec(memory_space=pl.ANY)
    block = (nc, rows // nc, features)
    parts = (ns, rows // nc, features // ns)
    micros, half, _ = out.shape
    return attend_back(
        functools.partial(attend_back_one, nc=nc), qx, k, v, grad_mixed, mixed, width, micro,
        [dw, dw, extra, out],
        [anywhere, once((1, main, features)), once(extra.shape), anywhere],
        [jax.ShapeDtypeStruct(parts, BF16), jax.ShapeDtypeStruct((micros, 2, half, features), BF16)],
        [full_spec(parts), anywhere],
        [
            pltpu.VMEM((rows, features), BF16), pltpu.VMEM((rows, features), BF16), pltpu.VMEM(block, BF16),
            *axis_sems(2, nc), pltpu.SemaphoreType.DMA((3,)),
        ],
        3,
    )


def attend_back_inputs(qx, k, v, grad_mixed, mixed, width, micro, dw_parts, dn, ns, nc):
    _, size, part = dw_parts.shape
    half, features = dn.shape[2:]
    anywhere = pl.BlockSpec(memory_space=pl.ANY)
    block = pltpu.VMEM((nc, half, features), BF16)
    return attend_back(
        functools.partial(attend_back_two, nc=nc, ns=ns), qx, k, v, grad_mixed, mixed, width, micro,
        [dw_parts, dn, dn],
        [once(dw_parts.shape), anywhere, once((nc, 1, half, features))],
        [jax.ShapeDtypeStruct((nc, size, part), BF16), jax.ShapeDtypeStruct((half, features), F32)],
        [full_spec((nc, size, part)), full_spec((half, features))],
        [
            pltpu.VMEM(dw_parts.shape, BF16), pltpu.VMEM((nc, size, part), BF16), block, block, block,
            *axis_sems(ns, nc, nc, nc),
        ],
        4,
    )


def ffn_kernel(
    x_ref, o_ref, g_ref, w_out, w_up, w_down, bup_ref, vec_ref,
    out_ref, gm_ref, gx_ref, dw_ref, dup_ref, dvec_ref, dw_acc,
):
    step = pl.program_id(0)
    steps = pl.num_programs(0)
    b_out, b_down, gain, shift = (vec_ref[i : i + 1, :] for i in range(4))
    hw = w_out.shape[1]
    hidden = w_up.shape[2]

    @pl.when(step == 0)
    def _():
        dw_acc[...] = jnp.zeros_like(dw_acc)
        dup_ref[...] = jnp.zeros_like(dup_ref)
        dvec_ref[...] = jnp.zeros_like(dvec_ref)

    mixed = o_ref[...]
    grad_b = g_ref[...]
    grad = grad_b.astype(F32)
    attended = dot_nn(mixed[:, :hw], w_out[0]) + dot_nn(mixed[:, hw:], w_out[1])
    middle = x_ref[...].astype(F32) + (attended + b_out)
    unit, inverse = unit_norm(middle)
    normed = (unit * gain + shift).astype(BF16)
    ffn_out = jnp.zeros_like(middle)
    grad_normed = jnp.zeros_like(middle)
    for part in range(2):
        pre = dot_nn(normed, w_up[part]) + bup_ref[part]
        gate = 0.5 + 0.5 * lax.erf(pre * math.sqrt(0.5))
        active = (pre * gate).astype(BF16)
        ffn_out += dot_nn(active, w_down[part])
        slope = gate + pre * jnp.exp(pre * pre * -0.5) * (1.0 / math.sqrt(2.0 * math.pi))
        grad_pre_f = dot_nt(grad_b, w_down[part]) * slope
        grad_pre = grad_pre_f.astype(BF16)
        dup_ref[part] += column_sum(grad_pre.astype(F32))
        grad_normed += dot_nt(grad_pre, w_up[part])
        dw_acc[part, hw : hw + hidden] += dot_tn(active, grad_b)
        dw_acc[part, hw + hidden :] += dot_tn(grad_pre, normed)
    out_ref[...] = (middle + (ffn_out + b_down)).astype(BF16)
    grad_middle = grad + norm_back(grad_normed, unit, inverse, gain)
    gm_ref[...] = grad_middle
    grad_att = grad_middle.astype(BF16)
    dvec_ref[0:1] += column_sum(grad_att.astype(F32))
    dvec_ref[1:2] += column_sum(grad)
    dvec_ref[2:3] += column_sum(grad_normed * unit)
    dvec_ref[3:4] += column_sum(grad_normed)
    for part in range(2):
        cols = slice(part * hw, (part + 1) * hw)
        gx_ref[:, cols] = dot_nt(grad_att, w_out[part]).astype(BF16)
        dw_acc[part, :hw] += dot_tn(mixed[:, cols], grad_att)

    @pl.when(step == steps - 1)
    def _():
        dw_ref[...] = dw_acc[...].astype(BF16)


def feed_forward(x, mixed, grad, w_out, w_up, w_down, b_up, vectors):
    rows, features = x.shape
    block = 256
    hw, hidden = w_out.shape[1], w_up.shape[2]
    total = hw + 2 * hidden
    row_spec = pl.BlockSpec((block, features), lambda i: (i, 0))

    def fixed(shape):
        return pl.BlockSpec(shape, lambda i: (0,) * len(shape), pipeline_mode=pl.Buffered(1))

    return pl.pallas_call(
        ffn_kernel,
        grid=(rows // block,),
        in_specs=[row_spec] * 3
        + [fixed(w.shape) for w in (w_out, w_up, w_down)]
        + [fixed(b_up.shape), fixed(vectors.shape)],
        out_specs=[row_spec] * 3
        + [full_spec((2, total, features)), full_spec((2, 1, hidden)), full_spec((8, features))],
        out_shape=[
            jax.ShapeDtypeStruct((rows, features), BF16),
            jax.ShapeDtypeStruct((rows, features), F32),
            jax.ShapeDtypeStruct((rows, 2 * hw), BF16),
            jax.ShapeDtypeStruct((2, total, features), BF16),
            jax.ShapeDtypeStruct((2, 1, hidden), F32),
            jax.ShapeDtypeStruct((8, features), F32),
        ],
        scratch_shapes=[pltpu.VMEM((2, total, features), F32)],
        compiler_params=params(),
        cost_estimate=pl.CostEstimate(
            flops=12 * rows * total * features, bytes_accessed=20 * total * features, transcendentals=4 * rows * hidden
        ),
        name="feed_forward",
    )(x, mixed, grad, w_out, w_up, w_down, b_up, vectors)


def back_kernel(x_ref, n_ref, dk_ref, dv_ref, dq_ref, w_ref, dw_start, db_start, dn_ref, dw_ref, db_ref, dw_acc):
    step = pl.program_id(0)
    width = w_ref.shape[3]
    normed = n_ref[...]
    unit, _ = unit_norm(x_ref[...].astype(F32))
    total = jnp.zeros(n_ref.shape, F32)

    @pl.when(step == 0)
    def _():
        dw_acc[...] = dw_start[...]
        db_ref[...] = db_start[...]
        query = jnp.zeros(n_ref.shape, F32)
        grad = dq_ref[...]
        for part in range(2):
            cols = slice(part * width, (part + 1) * width)
            dw_acc[part, 0] += dot_tn(grad[:, cols], normed)
            query += dot_nt(grad[:, cols], w_ref[part, 0])
        db_ref[0:1] += column_sum(grad.astype(F32))
        db_ref[2:3] += column_sum(query * unit)
        db_ref[3:4] += column_sum(query)
        dn_ref[...] = query.astype(BF16)

    for kind, ref in ((1, dk_ref), (2, dv_ref)):
        for part in range(2):
            cols = slice(part * width, (part + 1) * width)
            grad = ref[:, cols]
            total += dot_nt(grad, w_ref[part, kind])
            dw_acc[part, kind] += dot_tn(grad, normed)
    db_ref[1:2] += column_sum(dv_ref[...].astype(F32))
    db_ref[2:3] += column_sum(total * unit)
    db_ref[3:4] += column_sum(total)

    @pl.when(step == 0)
    def _():
        dn_ref[...] = (total + dn_ref[...].astype(F32)).astype(BF16)

    @pl.when(step > 0)
    def _():
        dn_ref[...] = total.astype(BF16)

    @pl.when(step == pl.num_programs(0) - 1)
    def _():
        dw_ref[...] = dw_acc[...].astype(dw_ref.dtype)


def project_back(x_all, normed, dq, dk, dv, weights, dw_start, db_start, kind):
    keys, features = normed.shape
    block = keys // 8
    width = weights.shape[3]
    stack = (2, 3, width, features)
    return pl.pallas_call(
        back_kernel,
        grid=(8,),
        in_specs=[
            pl.BlockSpec((block, features), lambda i: (i, 0)),
            pl.BlockSpec((block, features), lambda i: (i, 0)),
            pl.BlockSpec((block, 2 * width), lambda i: (i, 0)),
            pl.BlockSpec((block, 2 * width), lambda i: (i, 0)),
            once((block, 2 * width)),
            once(weights.shape),
            once(stack),
            once((8, 2 * width)),
        ],
        out_specs=[
            pl.BlockSpec((block, features), lambda i: (i, 0)),
            full_spec(stack),
            full_spec((8, 2 * width)),
        ],
        out_shape=[
            jax.ShapeDtypeStruct((keys, features), BF16),
            jax.ShapeDtypeStruct(stack, kind),
            jax.ShapeDtypeStruct((8, 2 * width), F32),
        ],
        scratch_shapes=[pltpu.VMEM(stack, F32)],
        compiler_params=params(),
        cost_estimate=pl.CostEstimate(
            flops=16 * keys * features * width, bytes_accessed=8 * keys * features, transcendentals=0
        ),
        name="project_back",
    )(x_all, normed, dk, dv, dq, weights, dw_start, db_start)


def last_kernel(
    dn_ref, dw_ref, extra_ref, dn_first, x_ref, gm_ref, gain_ref,
    grad_ref, blocks_ref,
    w_received, w_total, w_blocks, z_parts, z_received, dn_received, dn_total, dn_blocks,
    wtp_out, wtp_in, wctx_out, wctx_in, z_out, z_in, back_out, back_in, tp_out, tp_in, ctx_out, ctx_in,
    row_out, row_in, *, ns, nc,
):
    t = lax.axis_index("tp")
    micros, _, half, _ = grad_ref.shape
    rows = RowSum(
        dw_ref.at[1], dw_ref.at[0], extra_ref, w_received, w_total, w_blocks, (wtp_out, wtp_in),
        Axis("ctx", nc, (wctx_out, wctx_in)),
    )
    weights = ShardSum(
        z_parts, z_received, blocks_ref, Axis("shard", ns, (z_out, z_in)), Axis("ctx", nc, (back_out, back_in))
    )
    inputs = InputSum(
        lambda d: dn_ref.at[d, 1], lambda d: dn_ref.at[d, 0], dn_received, dn_total, dn_blocks,
        (tp_out, tp_in), Axis("ctx", nc, (ctx_out, ctx_in)),
    )

    def row(micro):
        return cross(grad_ref.at[micro, t], grad_ref.at[micro, t], (row_out, row_in), micro)

    def finish_rows(micro, grad_rows):
        size = 64

        def one(i, carry):
            at = pl.multiple_of(i * size, size)
            unit, inverse = unit_norm(x_ref[micro, pl.ds(at, size), :].astype(F32))
            value = gm_ref[micro, pl.ds(at, size), :] + norm_back(grad_rows(at, size), unit, inverse, gain_ref[...])
            grad_ref[micro, t, pl.ds(at, size), :] = value.astype(BF16)
            return carry

        lax.fori_loop(0, half // size, one, 0)
        row(micro).start()

    greet([("tp", 2), ("ctx", nc), ("shard", ns)])
    rows.start()
    inputs.start()
    rows.spread()
    inputs.spread()
    for micro in range(micros - 1):
        finish_rows(micro, lambda at, size: dn_first[micro, pl.ds(at, size), :])
    rows.finish(z_parts)
    weights.start()
    weights.spread()
    inputs.finish()
    finish_rows(micros - 1, inputs.rows)
    weights.finish()
    for micro in range(micros):
        row(micro).wait()


def last_sums(dn, dw, extra, dn_first, x, grad_middle, gain, ns, nc):
    main, features = dw.shape[1:]
    rows = main + extra.shape[1]
    micros, half, _ = x.shape
    size, part = rows // nc, features // ns
    block = pltpu.VMEM((nc, half, features), BF16)
    return pl.pallas_call(
        functools.partial(last_kernel, ns=ns, nc=nc),
        in_specs=[pl.BlockSpec(memory_space=pltpu.VMEM)] * 7,
        out_specs=[pl.BlockSpec(memory_space=pltpu.VMEM)] * 2,
        out_shape=[
            jax.ShapeDtypeStruct((micros, 2, half, features), BF16),
            jax.ShapeDtypeStruct((nc, size, part), BF16),
        ],
        scratch_shapes=[
            pltpu.VMEM((rows, features), BF16), pltpu.VMEM((rows, features), BF16), pltpu.VMEM((nc, size, features), BF16),
            pltpu.VMEM((ns, size, part), BF16), pltpu.VMEM((ns, size, part), BF16), block, block, block,
            *axis_sems(2, nc, ns, nc, nc, nc, micros),
        ],
        compiler_params=params(collective_id=5, has_side_effects=True),
        name="last_sums",
    )(dn, dw, extra, dn_first, x, grad_middle, gain)


def pad_rows(rows, multiple):
    extra = -rows.shape[0] % multiple
    return jnp.concatenate([rows, jnp.zeros((extra,) + rows.shape[1:], rows.dtype)]) if extra else rows


def body(
    tokens, cotangent, w_query, w_key, w_value, w_out, w_up, w_down,
    b_query, b_value, b_up, b_out, b_down, gain_attn, shift_attn, gain_ffn, shift_ffn,
):
    ns, nc = lax.axis_size("shard"), lax.axis_size("ctx")
    t = lax.axis_index("tp")
    micros, _, length, features = tokens.shape
    half = length // 2
    heads, head_part = b_query.shape
    head_width = head_part * ns
    up_part = b_up.shape[1]
    feature_part = b_out.shape[0]

    smalls = [b_query, b_value, b_up, b_out, b_down, gain_attn, shift_attn, gain_ffn, shift_ffn]
    flat = jnp.concatenate([v.reshape(-1) for v in smalls])
    small = jnp.pad(flat, (0, -flat.shape[0] % 2048)).reshape(-1, 128)
    w_all, small_all, x_first = gather_first(
        jnp.stack([w_query, w_key, w_value]), small, tokens[0, 0], ns, nc
    )
    small_all = small_all.reshape(2, ns, -1)
    offset = 0
    vectors = []
    for v in smalls:
        vectors.append(small_all[:, :, offset : offset + v.size])
        offset += v.size

    def by_head(v, part):
        return v.reshape(2, ns, heads, part).transpose(0, 2, 1, 3).reshape(2, heads * part * ns).astype(F32)

    def plain(v):
        return v[0].reshape(1, features).astype(F32)

    bq = by_head(vectors[0], head_part).reshape(1, -1)
    bv = by_head(vectors[1], head_part).reshape(1, -1)
    bup = by_head(vectors[2], up_part)[:, None, :]
    v_out, v_down, g_one, s_one, g_two, s_two = (plain(v) for v in vectors[3:])

    mine = lax.dynamic_slice_in_dim(tokens[:, 0], t * half, half, 1)
    grad_mine = lax.dynamic_slice_in_dim(cotangent[:, 0], t * half, half, 1)
    keys = 2 * nc * half
    aligned = feature_part % 128 == 0
    column_place = place_columns if aligned else place_slot

    def column_shape(w):
        return (2, w.shape[0], features) if aligned else (2, ns) + w.shape

    def whole_columns(w):
        if not aligned:
            w = w.transpose(0, 2, 1, 3).reshape(2, w.shape[2], features)
        return w

    plans = [
        (("ctx", nc, place_distance, True), ("shard", ns, place_rows, False), ("shard", ns, column_place, False)),
        (("shard", ns, column_place, False),),
    ]
    sources = [(tokens[1, 0], w_up, w_out), (w_down,)]
    shapes = [
        ((nc, 2, half, features), (2, features, w_up.shape[1]), column_shape(w_out)),
        (column_shape(w_down),),
    ]
    x_alls = [x_first.reshape(keys, features), None]
    saved = []
    arrived = []
    for micro in range(micros):
        normed, k, v, q = front(x_alls[micro], w_all, g_one, s_one, bq, bv, head_width)
        mixed, qx, *more = attend_forward(
            q, k, v, head_width, plans[micro], sources[micro], shapes[micro], micro + 1
        )
        if micro == 0:
            x_alls[1] = more.pop(0).reshape(keys, features)
        arrived += more
        saved.append((normed, k, v, qx, mixed))
    wu, wo, wd = arrived[0], whole_columns(arrived[1]), whole_columns(arrived[2])

    out, grad_middle, grad_mixed, dw, dup, dvec = feed_forward(
        mine.reshape(-1, features),
        jnp.concatenate([entry[4] for entry in saved]),
        grad_mine.reshape(-1, features),
        wo, wu, wd, bup, jnp.concatenate([v_out, v_down, g_two, s_two] * 2),
    )

    def spread(v, part):
        return v.reshape(heads, ns, part).transpose(1, 0, 2).reshape(ns, -1)

    def as_rows(v):
        count = v.shape[1] // feature_part
        return v.reshape(ns, count, feature_part).transpose(1, 0, 2).reshape(count, features)

    extra = jnp.stack(
        [pad_rows(jnp.concatenate([dvec[:4], as_rows(spread(dup[part, 0], up_part))]), 16 * nc) for part in range(2)]
    ).astype(BF16)

    width = heads * head_width
    normed, k, v, qx, mixed = saved[0]
    dq, dk, dv, dw_parts, output = attend_back_rows(
        qx, k, v, grad_mixed, mixed, head_width, 0, dw, extra, out.reshape(micros, half, features), ns, nc
    )
    start_dw = jnp.zeros((2, 3, width, features), F32)
    start_db = jnp.zeros((8, 2 * width), F32)
    dn, dw_now, db_now = project_back(x_alls[0], normed, dq, dk, dv, w_all, start_dw, start_db, F32)
    normed, k, v, qx, mixed = saved[1]
    dq, dk, dv, dw_done, dn_first = attend_back_inputs(
        qx, k, v, grad_mixed, mixed, head_width, 1, dw_parts, dn.reshape(nc, 2, half, features), ns, nc
    )
    dn, dw_now, db_now = project_back(x_alls[1], normed, dq, dk, dv, w_all, dw_now, db_now, BF16)

    extras = []
    for part in range(2):
        cols = slice(part * width, (part + 1) * width)
        biases = jnp.concatenate([spread(db_now[0, cols], head_part), spread(db_now[1, cols], head_part)], axis=1)
        extras.append(pad_rows(jnp.concatenate([db_now[2:4], as_rows(biases)]), 16 * nc))
    grad_tokens, attn_done = last_sums(
        dn.reshape(nc, 2, half, features), dw_now.reshape(2, 3 * width, features), jnp.stack(extras).astype(BF16),
        dn_first[None], mine, grad_middle.reshape(micros, half, features), g_one, ns, nc,
    )

    output = output.reshape(micros, 1, length, features)
    grad_tokens = grad_tokens.reshape(micros, 1, length, features)
    done_ffn = dw_done.reshape(-1, feature_part).astype(F32)
    done_attn = attn_done.reshape(-1, feature_part).astype(F32)
    hidden = heads * up_part * ns
    g_out, g_down, g_up = done_ffn[:width], done_ffn[width : width + hidden], done_ffn[width + hidden : width + 2 * hidden]
    tail = done_ffn[width + 2 * hidden :]
    g_query, g_key, g_value = (done_attn[i * width : (i + 1) * width].T for i in range(3))
    tail_attn = done_attn[3 * width :]
    g_bup = tail[4:].reshape(-1)[: heads * up_part].reshape(heads, up_part)
    g_heads = tail_attn[2:].reshape(-1)
    g_bq = g_heads[: heads * head_part].reshape(heads, head_part)
    g_bv = g_heads[heads * head_part : 2 * heads * head_part].reshape(heads, head_part)
    return (
        output, grad_tokens, g_query, g_key, g_value, g_out, g_up.T, g_down, g_bq, g_bv, g_bup,
        tail[0], tail[1], tail_attn[0], tail_attn[1], tail[2], tail[3],
    )


def solution(mesh):
    wide, tall = P("shard", "tp"), P("tp", "shard")
    rows, vector = P(None, "shard", "ctx", None), P("shard")
    weights = (wide, wide, wide, tall, wide, tall)
    return jax.shard_map(
        body,
        mesh=mesh,
        in_specs=(rows, rows) + weights + (tall,) * 3 + (vector,) * 6,
        out_specs=(rows, rows) + weights + (tall,) * 3 + (vector,) * 6,
        check_vma=False,
    )
```

time: 1320 us -> 394 us (0.30)
  matrix products: 497 us -> 0 us
  Pallas kernels: 0 us -> 349 us
  waiting for transfers between devices: 348 us -> 0 us
  other arithmetic: 226 us -> 8.48 us
  blocking collectives: 160 us -> 0 us
  local copies, waits for them, and re-layouts: 65.7 us -> 27.5 us
  between operations: 18.4 us -> 1.2 us
    dot_general x64 -> x0, matrix products: 497 us -> none  [the longest x8 106 us: one_block(): jnp.einsum('qhd,khd->hqk', query_block, key_heads, preferred_element_type...]
    pallas_call x0 -> x11, Pallas kernels: none -> 349 us  [the longest x2 96.7 us: attend_back(): pl.pallas_call(functools.partial(kernel, width=width), grid=(cols // lane...]
    reduce_scatter x8 -> x0, waiting for transfers between devices: 155 us -> none  [the longest x2 71.7 us: body(): lax.psum_scatter(grad_keys_all.astype(jnp.bfloat16), 'ctx', scatter_dimen...]
    convert_element_type x39 -> x4, other arithmetic: 140 us -> 1.22 us  [the longest x1 1.02 us: body(): done_attn = attn_done.reshape(-1, feature_part).astype(F32)]
    all_gather x13 -> x0, blocking collectives: 138 us -> none  [the longest x1 14.1 us: gather_weights(): lax.all_gather(w_key, 'shard', axis=0, tiled=True)]
    psum x4 -> x0, waiting for transfers between devices: 111 us -> none  [the longest x1 50.8 us: reduce_end(): lax.psum(p_query.astype(jnp.bfloat16), 'ctx').astype(jnp.float32)]
    reduce_sum x16 -> x0, other arithmetic: 76.3 us -> none  [the longest x4 56.4 us: one_block(): row_total = jnp.sum(exponent, axis=-1, keepdims=True)]
    unnamed x28 -> x0, waiting for transfers between devices: 75.7 us -> none
  transfers between devices with their start and end apart: 23 -> 0, of which waited for: 16 -> 0; matrix products, arithmetic and copies ran while one was open for 32% -> 0% of each run, Pallas kernels for 0% -> 0%
where the time goes in v1:
time: 394 us; the launch traced here: 386 us
  Pallas kernels  349 us (89%)
  local copies, waits for them, and re-layouts  27.5 us (7%)
  other arithmetic  8.48 us (2%)
    pallas_call x2, Pallas kernels, attend_back(): pl.pallas_call(functools.partial(kernel, width=width), grid=(cols // lane...  96.7 us
    pallas_call x2, Pallas kernels, attend_forward(): pl.pallas_call(functools.partial(attend_kernel, kc=kc, width=width, plans...  78.6 us
    pallas_call x1, Pallas kernels, last_sums(): pl.pallas_call(functools.partial(last_kernel, ns=ns, nc=nc), in_specs=[pl...  47.8 us
    pallas_call x2, Pallas kernels, project_back(): pl.pallas_call(back_kernel, grid=(8,), in_specs=[pl.BlockSpec((block, fea...  40.3 us
    pallas_call x1, Pallas kernels, gather_first(): pl.pallas_call(functools.partial(gather_kernel, ns, nc), in_specs=[pl.Blo...  34.2 us
    pallas_call x2, Pallas kernels, front(): pl.pallas_call(functools.partial(front_kernel, q_scale=LOG2E / math.sqrt(...  26.2 us
    pallas_call x1, Pallas kernels, feed_forward(): pl.pallas_call(ffn_kernel, grid=(rows // block,), in_specs=[row_spec] * 3...  25.2 us
    unnamed x42, local copies, waits for them, and re-layouts  8.05 us

profile of v1, /device:TPU:0, one launch (start us, length us, event | category | flops | bytes accessed | tf_op | source)
XLA Modules:
  0.0 386.2 jit_solution(9751364038536426634)
XLA Ops:
  0.8 3.1 slice_bitcast_fusion
  3.9 0.7 pad_maximum_fusion.1.w_ref
  5.6 34.2 %gather_first.1 = (bf16[2,3,512,256]{3,2,1,0:T(8,128)(2,1)}, bf16[2,4,16,128]{3,2,1,0:T(8,128)(2,1)}, bf16[4,2,512,512]{3,2,1,0:T(8,128)(2,1)}) custom-call(bf16[3,128,256]{2,1,0:T(8,128)(2,1)} %pad_maximum_fusion.1.w_ref, bf16[16,128]{1,0:T(8,128)(2,1)} %pad_bitcast_fusion.small_ref, bf16[1024,512]{1,0:T(8,128)(2,1)} %get-tuple-element.144.x_ref), custom_call_target="tpu_custom_call" | custom-call | tf_op jit(solution)/shard_map/gather_first/pallas_call | solution.py:134
  39.8 0.8 reshape.268
  41.3 0.7 reshape.288.bq_ref
  42.8 13.1 %front.2 = (bf16[4096,512]{1,0:T(8,128)(2,1)}, bf16[4096,512]{1,0:T(8,128)(2,1)}, bf16[4096,512]{1,0:T(8,128)(2,1)}, bf16[512,512]{1,0:T(8,128)(2,1)}) custom-call(bf16[4096,512]{1,0:T(8,128)(2,1)} %bitcast.147, bf16[2,3,512,256]{3,2,1,0:T(8,128)(2,1)} %get-tuple-element.61.w_ref, f32[1,512]{1,0:T(1,128)} %bitcast.142, f32[1,512]{1,0:T(1,128)} %bitcast.145, ...), custom_call_target="tpu_custom_call" | custom-call | flops 4294967296 | bytes 16777216 | tf_op jit(solution)/shard_map/front/pallas_call | solution.py:172
  55.8 46.7 %attend_forward.2 = (bf16[512,512]{1,0:T(8,128)(2,1)}, bf16[512,1024]{1,0:T(8,128)(2,1)}, bf16[4,2,512,512]{3,2,1,0:T(8,128)(2,1)}, bf16[2,512,1024]{2,1,0:T(8,128)(2,1)}, bf16[2,256,512]{2,1,0:T(8,128)(2,1)}) custom-call(bf16[512,512]{1,0:T(8,128)(2,1)} %get-tuple-element.63.refs_0_, bf16[4096,512]{1,0:T(8,128)(2,1)} %get-tuple-element.64.refs_1_.k_ref, ...), custom_call_target="tpu_custom_call" | custom-call | flops 12884901888 | bytes 8388608 | tf_op jit(solution)/shard_map/attend_forward/pallas_call | solution.py:390
  102.5 13.1 %front.3 = (bf16[4096,512]{1,0:T(8,128)(2,1)}, bf16[4096,512]{1,0:T(8,128)(2,1)}, bf16[4096,512]{1,0:T(8,128)(2,1)}, bf16[512,512]{1,0:T(8,128)(2,1)}) custom-call(bf16[4096,512]{1,0:T(8,128)(2,1)} %bitcast.149, bf16[2,3,512,256]{3,2,1,0:T(8,128)(2,1)} %get-tuple-element.61.w_ref, f32[1,512]{1,0:T(1,128)} %bitcast.143, f32[1,512]{1,0:T(1,128)} %bitcast.146, ...), custom_call_target="tpu_custom_call" | custom-call | flops 4294967296 | bytes 16777216 | tf_op jit(solution)/shard_map/front/pallas_call | solution.py:172
  115.7 31.9 %attend_forward.3 = (bf16[512,512]{1,0:T(8,128)(2,1)}, bf16[512,1024]{1,0:T(8,128)(2,1)}, bf16[2,1024,512]{2,1,0:T(8,128)(2,1)}) custom-call(bf16[512,512]{1,0:T(8,128)(2,1)} %get-tuple-element.69.refs_0_, bf16[4096,512]{1,0:T(8,128)(2,1)} %get-tuple-element.70.refs_1_.k_ref, bf16[4096,512]{1,0:T(8,128)(2,1)} %get-tuple-element.71.refs_2_.v_ref, ...), custom_call_target="tpu_custom_call" | custom-call | flops 12884901888 | bytes 8388608 | tf_op jit(solution)/shard_map/attend_forward/pallas_call | solution.py:390
  147.6 2.3 pad_maximum_fusion.o_ref
  150.6 2.7 constant_dynamic-slice_fusion
  153.4 0.7 reshape.290.bup_ref
  154.1 25.2 %feed_forward.1 = (bf16[1024,512]{1,0:T(8,128)(2,1)}, f32[1024,512]{1,0:T(8,128)}, bf16[1024,512]{1,0:T(8,128)(2,1)}, bf16[2,2304,512]{2,1,0:T(8,128)(2,1)}, f32[2,1,1024]{2,1,0:T(1,128)}, /*index=5*/f32[8,512]{1,0:T(8,128)}) custom-call(bf16[1024,512]{1,0:T(8,128)(2,1)} %bitcast.115, bf16[1024,512]{1,0:T(8,128)(2,1)} %pad_maximum_fusion.o_ref, ...), custom_call_target="tpu_custom_call" | custom-call | flops 14495514624 | bytes 23592960 | tf_op jit(solution)/shard_map/feed_forward/pallas_call | solution.py:824
  179.3 0.7 convert.85
  180.4 0.7 slice.235
  182.0 47.6 %attend_back.2 = (bf16[512,512]{1,0:T(8,128)(2,1)}, bf16[4096,512]{1,0:T(8,128)(2,1)}, bf16[4096,512]{1,0:T(8,128)(2,1)}, bf16[4,592,128]{2,1,0:T(8,128)(2,1)}, bf16[2,2,512,512]{3,2,1,0:T(8,128)(2,1)}) custom-call(bf16[512,1024]{1,0:T(8,128)(2,1)} %get-tuple-element.66.qx_ref, bf16[4096,512]{1,0:T(8,128)(2,1)} %get-tuple-element.64.refs_1_.k_ref, ...), custom_call_target="tpu_custom_call" | custom-call | flops 32212254720 | bytes 16777216 | tf_op jit(solution)/shard_map/attend_back/pallas_call | solution.py:682
  229.6 2.0 broadcast_in_dim.10.dw_start
  232.3 20.4 %project_back.2 = (bf16[4096,512]{1,0:T(8,128)(2,1)}, f32[2,3,256,512]{3,2,1,0:T(8,128)}, f32[8,512]{1,0:T(8,128)}) custom-call(bf16[4096,512]{1,0:T(8,128)(2,1)} %bitcast.148, bf16[4096,512]{1,0:T(8,128)(2,1)} %get-tuple-element.85.n_ref, bf16[4096,512]{1,0:T(8,128)(2,1)} %get-tuple-element.86.dk_ref, bf16[4096,512]{1,0:T(8,128)(2,1)} %get-tuple-element.87.dv_ref, ...), custom_call_target="tpu_custom_call" | custom-call | flops 8589934592 | bytes 16777216 | tf_op jit(solution)/shard_map/project_back/pallas_call | solution.py:899
  252.6 49.1 %attend_back.3 = (bf16[512,512]{1,0:T(8,128)(2,1)}, bf16[4096,512]{1,0:T(8,128)(2,1)}, bf16[4096,512]{1,0:T(8,128)(2,1)}, bf16[4,592,128]{2,1,0:T(8,128)(2,1)}, f32[512,512]{1,0:T(8,128)}) custom-call(bf16[512,1024]{1,0:T(8,128)(2,1)} %get-tuple-element.83.qx_ref, bf16[4096,512]{1,0:T(8,128)(2,1)} %get-tuple-element.70.refs_1_.k_ref, ...), custom_call_target="tpu_custom_call" | custom-call | flops 32212254720 | bytes 16777216 | tf_op jit(solution)/shard_map/attend_back/pallas_call | solution.py:682
  301.7 19.9 %project_back.3 = (bf16[4096,512]{1,0:T(8,128)(2,1)}, bf16[2,3,256,512]{3,2,1,0:T(8,128)(2,1)}, f32[8,512]{1,0:T(8,128)}) custom-call(bf16[4096,512]{1,0:T(8,128)(2,1)} %bitcast.150, bf16[4096,512]{1,0:T(8,128)(2,1)} %get-tuple-element.82.n_ref, bf16[4096,512]{1,0:T(8,128)(2,1)} %get-tuple-element.90.dk_ref, bf16[4096,512]{1,0:T(8,128)(2,1)} %get-tuple-element.91.dv_ref, ...), custom_call_target="tpu_custom_call" | custom-call | flops 8589934592 | bytes 16777216 | tf_op jit(solution)/shard_map/project_back/pallas_call | solution.py:899
  321.6 0.7 convert.87
  323.3 0.7 slice.236
  324.9 47.8 %last_sums.1 = (bf16[2,2,512,512]{3,2,1,0:T(8,128)(2,1)}, bf16[4,208,128]{2,1,0:T(8,128)(2,1)}) custom-call(bf16[4,2,512,512]{3,2,1,0:T(8,128)(2,1)} %bitcast.114, bf16[2,768,512]{2,1,0:T(8,128)(2,1)} %bitcast.120, bf16[2,64,512]{2,1,0:T(8,128)(2,1)} %pad_maximum_fusion.3.extra_ref, f32[1,512,512]{2,1,0:T(8,128)} %bitcast.122, ...), custom_call_target="tpu_custom_call" | custom-call | tf_op jit(solution)/shard_map/last_sums/pallas_call | solution.py:991
  372.7 1.0 bitcast_convert_fusion.1
  373.7 0.8 copy.62
  374.5 0.8 copy.63
  375.3 0.8 copy.64
  377.4 1.0 fusion.8
  378.4 2.0 copy.61
  382.3 1.3 copy.91
  383.6 1.0 copy-done.2
  384.7 1.3 copy.92
  (95 shorter events, 10.1 us)
Async XLA Ops:
  0.7 3.2 copy-start.7
  0.7 3.2 copy-start.6
  0.7 3.2 copy-start.5
  0.7 3.9 %copy-start.14 = (bf16[4,16]{1,0:T(4,128)(2,1)S(1)}, bf16[4,16]{1,0:T(4,128)(2,1)}, u32[]{:S(2)}) copy-start(bf16[4,16]{1,0:T(4,128)(2,1)} %param.25) | copy-start | bytes 388
  0.7 4.0 %copy-start.15 = (bf16[4,16]{1,0:T(4,128)(2,1)S(1)}, bf16[4,16]{1,0:T(4,128)(2,1)}, u32[]{:S(2)}) copy-start(bf16[4,16]{1,0:T(4,128)(2,1)} %param.26) | copy-start | bytes 388
  0.7 4.1 %copy-start.16 = (bf16[4,64]{1,0:T(4,128)(2,1)S(1)}, bf16[4,64]{1,0:T(4,128)(2,1)}, u32[]{:S(2)}) copy-start(bf16[4,64]{1,0:T(4,128)(2,1)} %param.27) | copy-start | bytes 1540
  0.7 4.1 %copy-start.8 = (bf16[128]{0:T(256)(128)(2,1)S(1)}, bf16[128]{0:T(256)(128)(2,1)}, u32[]{:S(2)}) copy-start(bf16[128]{0:T(256)(128)(2,1)} %param.28) | copy-start | bytes 772
  0.7 4.1 %copy-start.9 = (bf16[128]{0:T(256)(128)(2,1)S(1)}, bf16[128]{0:T(256)(128)(2,1)}, u32[]{:S(2)}) copy-start(bf16[128]{0:T(256)(128)(2,1)} %param.29) | copy-start | bytes 772
  0.7 4.1 %copy-start.10 = (bf16[128]{0:T(256)(128)(2,1)S(1)}, bf16[128]{0:T(256)(128)(2,1)}, u32[]{:S(2)}) copy-start(bf16[128]{0:T(256)(128)(2,1)} %param.30) | copy-start | bytes 772
  0.7 4.1 %copy-start.11 = (bf16[128]{0:T(256)(128)(2,1)S(1)}, bf16[128]{0:T(256)(128)(2,1)}, u32[]{:S(2)}) copy-start(bf16[128]{0:T(256)(128)(2,1)} %param.31) | copy-start | bytes 772
  0.8 4.1 %copy-start.12 = (bf16[128]{0:T(256)(128)(2,1)S(1)}, bf16[128]{0:T(256)(128)(2,1)}, u32[]{:S(2)}) copy-start(bf16[128]{0:T(256)(128)(2,1)} %param.32) | copy-start | bytes 772
  0.8 4.1 %copy-start.13 = (bf16[128]{0:T(256)(128)(2,1)S(1)}, bf16[128]{0:T(256)(128)(2,1)}, u32[]{:S(2)}) copy-start(bf16[128]{0:T(256)(128)(2,1)} %param.33) | copy-start | bytes 772
  115.7 32.0 %copy-start.4 = (bf16[512,512]{1,0:T(8,128)(2,1)S(1)}, bf16[512,512]{1,0:T(8,128)(2,1)}, u32[]{:S(2)}) copy-start(bf16[512,512]{1,0:T(8,128)(2,1)} %get-tuple-element.67.o_ref) | copy-start | bytes 1572868
  147.6 3.0 copy-start
  372.7 4.6 %copy-start.3 = (bf16[4,592,128]{2,1,0:T(8,128)(2,1)S(1)}, bf16[4,592,128]{2,1,0:T(8,128)(2,1)}, u32[]{:S(2)}) copy-start(bf16[4,592,128]{2,1,0:T(8,128)(2,1)} %get-tuple-element.102) | copy-start | bytes 1818628
  377.4 4.9 %copy-start.1 = (bf16[2,2,512,512]{3,2,1,0:T(8,128)(2,1)S(1)}, bf16[2,2,512,512]{3,2,1,0:T(8,128)(2,1)}, u32[]{:S(2)}) copy-start(bf16[2,2,512,512]{3,2,1,0:T(8,128)(2,1)} %get-tuple-element.81) | copy-start | bytes 6291460
  382.3 2.3 copy-start.2
